TPU v7x, 32 devices: a whole 2x2x4 slice. The times are simulated.
32 devices in a mesh: dp: 8 (over z, y), db: 4 (over x, core).
Axes of the slice: x: 2, y: 2, z: 4, core: 2. Of those that a mesh axis runs over, the one named last changes fastest.
Arguments:
- queries: bfloat16 [8, 1024, 2048], P('dp', 'db'), may hold values from -6 to 6
- cotangent: bfloat16 [8, 1024, 2048], P('dp', 'db'), may hold values from -6 to 6
- w_key: bfloat16 [896, 2048], replicated, may hold values from -0.1875 to 0.1875
- w_value: bfloat16 [896, 2048], replicated, may hold values from -0.1875 to 0.1875
- database: bfloat16 [128, 128, 896], P('db'), may hold values from -6 to 6
- nb_shard: int32 [8, 16, 2], P('dp', 'db'), may hold values from 0 to 3, all different within a row; in each aligned block of 4 rows (0 to 3, 4 to 7, ..., all dimensions but the last counted through in order) at most 3 rows name the same one
- nb_row: int32 [8, 16, 2], P('dp', 'db'), may hold values from 0 to 31
Outputs:
- attn_out: bfloat16 [8, 1024, 2048], P('dp', 'db')
- grad_queries: bfloat16 [8, 1024, 2048], P('dp', 'db')
- grad_wkey: float32 [896, 2048], P(('dp', 'db'))
- grad_wvalue: float32 [896, 2048], P(('dp', 'db'))
- grad_database: bfloat16 [128, 128, 896], P('db', 'dp')
Inputs may be any that keep to these rules, and one draw needn't show every extreme that they name: `nb_shard`: the 2 neighbours of a stretch lie on different shards; among the stretches of one device (aligned blocks of 4 stretches of a sequence) at most 3 name the same shard, a bound that some block reaches.
All inputs are finite; a program needn't handle non-finite values.
Results may differ from a plain program's by a relative error of at most 0.015.
Values may be sent and summed in bfloat16 or wider, within the bound.
A program may use at most 192 MiB of HBM per device.

v0:
```python
import functools
import math

import jax
import jax.numpy as jnp
import numpy as np
from jax import lax
from jax.experimental import pallas as pl
from jax.experimental.pallas import tpu as pltpu
from jax.sharding import PartitionSpec as P

HSIZE = 128


def from_behind(block, axis, distance):
    devices = range(lax.axis_size(axis))
    route = [(i - distance, i) for i in devices if i - distance in devices]
    return lax.ppermute(block, axis, route)


def dot(a, b, dims):
    return lax.dot_general(a, b, (dims, ((), ())), preferred_element_type=jnp.float32)


def attend_kernel(scale, q_ref, g_ref, kv_ref, out_ref, dq_ref, both_ref):
    width = q_ref.shape[1]
    for head in range(width // HSIZE):
        cols = slice(head * HSIZE, (head + 1) * HSIZE)
        vcols = slice(width + head * HSIZE, width + (head + 1) * HSIZE)
        q = q_ref[:, cols]
        g = g_ref[:, cols]
        k = kv_ref[:, cols]
        v = kv_ref[:, vcols]
        scores = dot(q, k, ((1,), (1,))) * scale
        dprob = dot(g, v, ((1,), (1,)))
        expo = jnp.exp(scores - jnp.max(scores, axis=-1, keepdims=True))
        prob = expo * (1.0 / jnp.sum(expo, axis=-1, keepdims=True))
        prob_b = prob.astype(jnp.bfloat16)
        rowdot = jnp.sum(prob * dprob, axis=-1, keepdims=True)
        dscore = (prob * (dprob - rowdot) * scale).astype(jnp.bfloat16)
        out_ref[:, cols] = dot(prob_b, v, ((1,), (0,))).astype(jnp.bfloat16)
        dq_ref[:, cols] = dot(dscore, k, ((1,), (0,))).astype(jnp.bfloat16)
        both_ref[:, cols] = dot(dscore, q, ((0,), (0,))).astype(jnp.bfloat16)
        both_ref[:, vcols] = dot(prob_b, g, ((0,), (0,))).astype(jnp.bfloat16)


def attend(block_q, block_g, kv, stretches):
    rows, width = block_q.shape
    length = rows // stretches
    span = kv.shape[0] // stretches
    scale = 1.0 / math.sqrt(HSIZE)
    small = pl.BlockSpec((length, width), lambda u: (u, 0))
    large = pl.BlockSpec((span, 2 * width), lambda u: (u, 0))
    return pl.pallas_call(
        functools.partial(attend_kernel, scale),
        grid=(stretches,),
        in_specs=[small, small, large],
        out_specs=[small, small, large],
        out_shape=[
            jax.ShapeDtypeStruct((rows, width), jnp.bfloat16),
            jax.ShapeDtypeStruct((rows, width), jnp.bfloat16),
            jax.ShapeDtypeStruct(kv.shape, jnp.bfloat16),
        ],
        compiler_params=pltpu.CompilerParams(vmem_limit_bytes=40 << 20),
        cost_estimate=pl.CostEstimate(
            flops=12 * rows * span * width,
            bytes_accessed=8 * rows * width + 8 * kv.shape[0] * width,
            transcendentals=rows * span * width // HSIZE,
        ),
    )(block_q, block_g, kv)


def halve(block, axis, bit):
    size = lax.axis_size(axis)
    half = block.shape[0] // 2
    side = lax.rem(lax.axis_index(axis) // bit, 2)
    give = lax.dynamic_slice_in_dim(block, (1 - side) * half, half, 0)
    mine = lax.dynamic_slice_in_dim(block, side * half, half, 0)
    got = lax.ppermute(give, axis, [(i, i ^ bit) for i in range(size)])
    return mine.astype(jnp.float32) + got.astype(jnp.float32)


def bits_of(axis):
    size = lax.axis_size(axis)
    return [1 << b for b in range(size.bit_length() - 1)]


def halve_all(block, steps):
    for axis, bit in steps[:-1]:
        block = halve(block, axis, bit).astype(jnp.bfloat16)
    return halve(block, *steps[-1])


def reversed_order(count):
    bits = count.bit_length() - 1
    return np.array([int(format(i, "b").zfill(bits)[::-1], 2) if bits else 0 for i in range(count)])


def body(queries, cotangent, w_key, w_value, database, nb_shard, nb_row):
    q_local = queries[0]
    g_local = cotangent[0]
    rows_local, width = q_local.shape
    stretch_count = nb_shard.shape[1]
    neigh = nb_shard.shape[2]
    span = rows_local // stretch_count
    db_count, nb_len, enc_width = database.shape
    shards = lax.axis_size("db")
    seqs = lax.axis_size("dp")
    asks = stretch_count * neigh
    slot_count = 3 * asks // (2 * shards)
    target = nb_shard[0].reshape(asks)
    wanted = nb_row[0].reshape(asks)
    hits = (target[:, None] == jnp.arange(shards, dtype=jnp.int32)[None, :]).astype(jnp.int32)
    before = jnp.cumsum(hits, axis=0) - hits
    rank = jnp.sum(before * hits, axis=1)
    slot_pos = target * slot_count + rank
    place = (slot_pos[:, None] == jnp.arange(shards * slot_count, dtype=jnp.int32)[None, :]).astype(
        jnp.int32
    )
    send_ids = jnp.sum(place * wanted[:, None], axis=0).reshape(shards, slot_count)
    asked = lax.all_to_all(send_ids, "db", split_axis=0, concat_axis=0, tiled=True)
    picked = jnp.take(database, asked, axis=0)
    returned = lax.all_to_all(picked, "db", split_axis=0, concat_axis=0, tiled=True)

    ids = jnp.broadcast_to((target * db_count + wanted)[None], (seqs, asks))
    ids = lax.all_to_all(ids, "dp", split_axis=0, concat_axis=0, tiled=True).reshape(seqs * asks)
    member = (
        ids[None, :] == jnp.arange(shards * db_count, dtype=jnp.int32)[:, None]
    ).astype(jnp.bfloat16)

    next_q, next_g = from_behind((q_local[:span], g_local[:span]), "db", -1)
    block_q = jnp.concatenate([q_local[span - 1 :], next_q[: span - 1]], axis=0)
    block_g = jnp.concatenate([g_local[span - 1 :], next_g[: span - 1]], axis=0)
    w_both = jnp.concatenate([w_key, w_value], axis=1)

    devices = shards * seqs
    share = enc_width // devices
    source = (reversed_order(devices)[:, None] * share + np.arange(share)[None, :]).reshape(-1)
    shuffle = (
        jnp.arange(enc_width, dtype=jnp.int32)[:, None] == jnp.asarray(source, jnp.int32)[None, :]
    ).astype(jnp.bfloat16)

    states = jnp.take(returned.reshape(shards * slot_count, nb_len, enc_width), slot_pos, axis=0)
    states = states.reshape(asks * nb_len, enc_width)
    kv = dot(states, w_both, ((1,), (0,))).astype(jnp.bfloat16)
    shuffled = dot(states, shuffle, ((1,), (0,))).astype(jnp.bfloat16)
    outputs, dquery, both = attend(block_q, block_g, kv, stretch_count)

    steps = [("db", b) for b in bits_of("db")] + [("dp", b) for b in bits_of("dp")]
    grads = []
    for part in range(2):
        grad = dot(shuffled, both[:, part * width : (part + 1) * width], ((0,), (0,)))
        grads.append(halve_all(grad.astype(jnp.bfloat16), steps))

    keep = rows_local - span + 1
    prev_out, prev_dq = from_behind((outputs[keep:], dquery[keep:]), "db", 1)
    attn_out = jnp.concatenate([prev_out, outputs[:keep]], axis=0)[None]
    grad_queries = jnp.concatenate([prev_dq, dquery[:keep]], axis=0)[None]

    dstates = dot(both, w_both, ((1,), (1,))).astype(jnp.bfloat16)
    piece = nb_len // seqs
    dstates = dstates.reshape(asks, seqs, piece, enc_width).transpose(1, 0, 2, 3)
    arrived = lax.all_to_all(dstates, "dp", split_axis=0, concat_axis=0, tiled=True)
    dense = dot(member, arrived.reshape(seqs * asks, piece * enc_width), ((1,), (0,)))
    dense = dense.astype(jnp.bfloat16).reshape(shards, db_count, piece, enc_width)
    dense = dense[reversed_order(shards)]
    grad_database = halve_all(dense, [("db", b) for b in bits_of("db")])[0].astype(jnp.bfloat16)
    return (attn_out, grad_queries, grads[0], grads[1], grad_database)


def solution(mesh):
    return jax.shard_map(
        body,
        mesh=mesh,
        in_specs=(
            P("dp", "db", None),
            P("dp", "db", None),
            P(),
            P(),
            P("db", None, None),
            P("dp", "db", None),
            P("dp", "db", None),
        ),
        out_specs=(
            P("dp", "db", None),
            P("dp", "db", None),
            P(("dp", "db"), None),
            P(("dp", "db"), None),
            P("db", "dp", None),
        ),
        check_vma=False,
    )
```

profile of v0, /device:TPU:0, one launch (start us, length us, event | category | flops | bytes accessed | tf_op | source)
XLA Modules:
  0.0 261.2 jit_solution(143216100373839621)
XLA Ops:
  0.6 1.0 slice_bitcast_fusion.3
  1.6 1.3 collective-permute-start
  2.9 1.0 slice_bitcast_fusion.2
  3.9 1.3 collective-permute-start.1
  5.2 0.8 copy.34
  6.0 0.8 copy.33
  7.2 0.7 all_to_all.20
  7.9 6.3 %all-to-all-start = ((s32[4,1,3]{2,1,0:T(1,128)}), s32[4,1,3]{2,1,0:T(1,128)S(1)}, u32[]{:S(2)}, u32[]{:S(2)}) async-start(s32[4,1,3]{2,1,0:T(1,128)} %bitcast.5), calls=%async_computation | async-start | bytes 4096 | tf_op jit(solution)/shard_map/all_to_all | solution.py:121
  14.2 4.6 %constant_dynamic-update-slice_fusion.1 = bf16[896,4096]{1,0:T(8,128)(2,1)} fusion(bf16[896,2048]{1,0:T(8,128)(2,1)} %param.12), kind=kLoop, calls=%fused_computation.60 | loop fusion | bytes 7340032
  18.8 2.4 constant_dynamic-update-slice_fusion
  21.1 0.6 broadcast_in_dim.53
  21.7 5.8 %all-to-all-start.2 = ((s32[8,1,8]{2,1,0:T(1,128)}), s32[8,1,8]{2,1,0:T(1,128)S(1)}, u32[]{:S(2)}, u32[]{:S(2)}) async-start(s32[8,1,8]{2,1,0:T(1,128)} %broadcast_in_dim.53), calls=%async_computation.2 | async-start | bytes 8192 | tf_op jit(solution)/shard_map/all_to_all | solution.py:126
  27.9 4.2 %gather_fusion = bf16[12,128,896]{2,1,0:T(8,128)(2,1)S(1)} fusion(bf16[32,128,896]{2,1,0:T(8,128)(2,1)} %param.14, s32[1024]{0:T(1024)S(1)} %get-tuple-element.14), kind=kCustom, calls=%fused_computation | custom fusion | bytes 5505072 | tf_op jit(solution)/shard_map/jit(_take)/gather | solution.py:122
  32.0 2.0 broadcast_select_fusion
  34.0 4.9 %all-to-all-start.1 = ((bf16[4,3,128,896]{3,2,1,0:T(8,128)(2,1)}), bf16[4,3,128,896]{3,2,1,0:T(8,128)(2,1)}, u32[]{:S(2)}, u32[]{:S(2)}) async-start(bf16[4,3,128,896]{3,2,1,0:T(8,128)(2,1)} %broadcast_select_fusion), calls=%async_computation.1 | async-start | bytes 5505024 | tf_op jit(solution)/shard_map/all_to_all | solution.py:123
  39.4 1.3 slice_bitcast_fusion
  40.9 0.5 broadcast.145
  41.4 0.7 reduce.3
  42.1 1.1 pad_maximum_fusion.q_ref
  43.2 1.1 pad_maximum_fusion.1.g_ref
  44.3 27.3 %all-to-all-done.1 = bf16[4,3,128,896]{3,2,1,0:T(8,128)(2,1)} async-done(((bf16[4,3,128,896]{3,2,1,0:T(8,128)(2,1)}), bf16[4,3,128,896]{3,2,1,0:T(8,128)(2,1)}, u32[]{:S(2)}, u32[]{:S(2)}) %all-to-all-start.1) | async-done | bytes 2752544 | tf_op jit(solution)/shard_map/all_to_all | solution.py:123
  71.7 3.8 %gather_fusion.1 = bf16[8,128,896]{2,1,0:T(8,128)(2,1)} fusion(bf16[12,128,896]{2,1,0:T(8,128)(2,1)} %bitcast.9, s32[1024]{0:T(1024)S(1)} %pad_clamp_fusion.1), kind=kCustom, calls=%fused_computation.1 | custom fusion | bytes 3670048 | tf_op jit(solution)/shard_map/jit(_take)/gather | solution.py:143
  75.4 1.8 bitcast_select_fusion
  77.2 13.9 %convolution_convert_fusion.1.kv_ref = bf16[1024,4096]{1,0:T(8,128)(2,1)} fusion(bf16[1024,896]{1,0:T(8,128)(2,1)S(1)} %bitcast_select_fusion, bf16[896,4096]{1,0:T(8,128)(2,1)} %constant_dynamic-update-slice_fusion), kind=kOutput, calls=%fused_computation.4 | convolution fusion | flops 7520387072 | bytes 17563648 | tf_op jit(solution)/shard_map/dot_general | solution.py:22
  91.2 2.3 fusion.11
  93.5 31.8 %shard_map.137 = (bf16[256,2048]{1,0:T(8,128)(2,1)S(1)}, bf16[256,2048]{1,0:T(8,128)(2,1)S(1)}, bf16[1024,4096]{1,0:T(8,128)(2,1)S(1)}) custom-call(bf16[256,2048]{1,0:T(8,128)(2,1)S(1)} %pad_maximum_fusion.q_ref, bf16[256,2048]{1,0:T(8,128)(2,1)S(1)} %pad_maximum_fusion.1.g_ref, bf16[1024,4096]{1,0:T(8,128)(2,1)} %convolution_convert_fusion.1.kv_ref), custom_call_target="tpu_custom_call" | custom-call | flops 1610612736 | bytes 20971520 | tf_op jit(solution)/shard_map/pallas_call | solution.py:54
  125.3 4.3 %fusion.4 = bf16[896,2048]{1,0:T(8,128)(2,1)S(1)} fusion(bf16[1024,896]{1,0:T(8,128)(2,1)S(1)} %fusion.11, bf16[1024,4096]{1,0:T(8,128)(2,1)S(1)} %get-tuple-element.10), kind=kOutput, calls=%fused_computation.12 | convolution fusion | flops 3759931392 | bytes 9699328 | tf_op jit(solution)/shard_map/dot_general | solution.py:22
  129.7 4.5 %fusion.7 = bf16[896,2048]{1,0:T(8,128)(2,1)S(1)} fusion(bf16[1024,896]{1,0:T(8,128)(2,1)S(1)} %fusion.11, bf16[1024,4096]{1,0:T(8,128)(2,1)S(1)} %get-tuple-element.10), kind=kOutput, calls=%fused_computation.13 | convolution fusion | flops 3759931392 | bytes 9699328 | tf_op jit(solution)/shard_map/dot_general | solution.py:22
  134.2 0.9 slice.58
  135.0 2.2 collective-permute-start.2
  137.2 1.5 constant_dynamic-slice_fusion.11
  138.9 1.4 constant_dynamic-slice_fusion.6
  140.7 11.3 %convolution_convert_fusion.2 = bf16[1024,896]{1,0:T(8,128)(2,1)S(1)} fusion(bf16[1024,4096]{1,0:T(8,128)(2,1)S(1)} %get-tuple-element.10, bf16[896,4096]{1,0:T(8,128)(2,1)} %constant_dynamic-update-slice_fusion), kind=kOutput, calls=%fused_computation.22 | convolution fusion | flops 7517110272 | bytes 17563648 | tf_op jit(solution)/shard_map/dot_general | solution.py:22
  152.0 0.8 slice.60
  152.8 2.8 %collective-permute-start.3 = (bf16[63,2048]{1,0:T(8,128)(2,1)}, bf16[63,2048]{1,0:T(8,128)(2,1)}, u32[]{:S(2)}, u32[]{:S(2)}) collective-permute-start(bf16[63,2048]{1,0:T(8,128)(2,1)} %slice.60), channel_id=1, source_target_pairs={{0,1},{1,2},{2,3},{4,5},{5,6},{6,7},{8,9},{9,10},{10,11},{12,13},{... | collective-permute-start | bytes 774152 | tf_op jit(solution)/shard_map/ppermute | solution.py:18
  155.6 1.4 copy.43
  157.0 6.0 %all-to-all-start.3 = ((bf16[8,8,16,896]{3,2,1,0:T(8,128)(2,1)}), bf16[8,8,16,896]{3,2,1,0:T(8,128)(2,1)S(1)}, u32[]{:S(2)}, u32[]{:S(2)}) async-start(bf16[8,8,16,896]{3,2,1,0:T(8,128)(2,1)} %bitcast.55), calls=%async_computation.3 | async-start | bytes 3670016 | tf_op jit(solution)/shard_map/all_to_all | solution.py:163
  163.0 2.1 maximum_bitcast_fusion
  165.2 3.0 %add_convert_fusion.2 = bf16[448,2048]{1,0:T(8,128)(2,1)S(1)} fusion(bf16[448,2048]{1,0:T(8,128)(2,1)} %collective-permute-done.4, bf16[896,2048]{1,0:T(8,128)(2,1)} %copy-done.4, s32[]{:T(128)S(6)} %select_n.122), kind=kLoop, calls=%fused_computation.11 | loop fusion | flops 3670016 | bytes 5505028 | tf_op jit(solution)/shard_map/convert_element_type | solution.py:90
  168.4 2.2 add_convert_fusion.1
  170.7 2.1 collective-permute-start.10
  172.7 2.1 maximum_bitcast_fusion.1
  174.8 16.8 %collective-permute-done.5 = bf16[224,2048]{1,0:T(8,128)(2,1)S(1)} collective-permute-done((bf16[224,2048]{1,0:T(8,128)(2,1)S(1)}, bf16[224,2048]{1,0:T(8,128)(2,1)S(1)}, u32[]{:S(2)}, u32[]{:S(2)}) %collective-permute-start.5) | collective-permute-done | bytes 917536 | tf_op jit(solution)/shard_map/ppermute | solution.py:79
  192.0 2.1 collective-permute-start.6
  194.1 15.2 %collective-permute-done.10 = bf16[224,2048]{1,0:T(8,128)(2,1)S(1)} collective-permute-done((bf16[224,2048]{1,0:T(8,128)(2,1)S(1)}, bf16[224,2048]{1,0:T(8,128)(2,1)S(1)}, u32[]{:S(2)}, u32[]{:S(2)}) %collective-permute-start.10) | collective-permute-done | bytes 917536 | tf_op jit(solution)/shard_map/ppermute | solution.py:79
  209.6 0.8 constant_dynamic-slice_fusion.4
  210.4 1.7 collective-permute-start.11
  212.3 0.7 constant_dynamic-slice_fusion.8
  213.0 1.5 collective-permute-start.7
  214.5 0.4 copy.40
  214.9 1.1 convolution_convert_fusion
  216.0 2.6 copy.41
  218.6 4.9 %gather_fusion.2 = bf16[4,32,16,896]{3,2,1,0:T(8,128)(2,1)} fusion(bf16[4,32,16,896]{3,2,1,0:T(8,128)(2,1)} %bitcast.52, s32[1024]{0:T(1024)S(1)} %get-tuple-element.13), kind=kCustom, calls=%fused_computation.2 | custom fusion | bytes 7340048 | tf_op jit(solution)/shard_map/gather | solution.py:166
  223.4 1.8 constant_dynamic-slice_fusion.1
  225.3 1.1 add_convert_fusion.6
  226.5 0.6 collective-permute-start.12
  227.3 2.4 collective-permute-start.8
  229.7 7.7 %collective-permute-done.12 = bf16[56,2048]{1,0:T(8,128)(2,1)S(1)} collective-permute-done((bf16[56,2048]{1,0:T(8,128)(2,1)S(1)}, bf16[56,2048]{1,0:T(8,128)(2,1)S(1)}, u32[]{:S(2)}, u32[]{:S(2)}) %collective-permute-start.12) | collective-permute-done | bytes 229408 | tf_op jit(solution)/shard_map/ppermute | solution.py:79
  237.5 0.5 add_convert_fusion
  238.8 0.8 convert_add_fusion.1
  239.6 7.1 %collective-permute-done.13 = bf16[28,2048]{1,0:T(8,128)(2,1)S(1)} collective-permute-done((bf16[28,2048]{1,0:T(8,128)(2,1)S(1)}, bf16[28,2048]{1,0:T(8,128)(2,1)S(1)}, u32[]{:S(2)}, u32[]{:S(2)}) %collective-permute-start.13) | collective-permute-done | bytes 114720 | tf_op jit(solution)/shard_map/ppermute | solution.py:79
  246.7 0.7 convert_add_fusion
  247.4 12.6 %collective-permute-done.15 = bf16[1,32,16,896]{3,2,1,0:T(8,128)(2,1)S(1)} collective-permute-done((bf16[1,32,16,896]{3,2,1,0:T(8,128)(2,1)S(1)}, bf16[1,32,16,896]{3,2,1,0:T(8,128)(2,1)S(1)}, u32[]{:S(2)}, u32[]{:S(2)}) %collective-permute-start.15) | collective-permute-done | bytes 917536 | tf_op jit(solution)/shard_map/ppermute | solution.py:79
  260.1 1.1 fusion.13
  (74 shorter events, 4.2 us)
Async XLA Ops:
  1.6 40.5 %collective-permute-start = (bf16[64,2048]{1,0:T(8,128)(2,1)S(1)}, bf16[64,2048]{1,0:T(8,128)(2,1)}, u32[]{:S(2)}, u32[]{:S(2)}) collective-permute-start(bf16[64,2048]{1,0:T(8,128)(2,1)S(1)} %slice_bitcast_fusion.3), channel_id=1, source_target_pairs={{1,0},{2,1},{3,2},{5,4},{6,5},{7,6},{9,8},{10,9},{11,10},{13,12},{... | collective-permute-start | bytes 786440 | tf_op jit(solution)/shard_map/ppermute | solution.py:18
  3.9 39.4 %collective-permute-start.1 = (bf16[64,2048]{1,0:T(8,128)(2,1)S(1)}, bf16[64,2048]{1,0:T(8,128)(2,1)}, u32[]{:S(2)}, u32[]{:S(2)}) collective-permute-start(bf16[64,2048]{1,0:T(8,128)(2,1)S(1)} %slice_bitcast_fusion.2), channel_id=1, source_target_pairs={{1,0},{2,1},{3,2},{5,4},{6,5},{7,6},{9,8},{10,9},{11,10},{13,12},{... | collective-permute-start | bytes 786440 | tf_op jit(solution)/shard_map/ppermute | solution.py:18
  7.9 13.3 %all-to-all-start = ((s32[4,1,3]{2,1,0:T(1,128)}), s32[4,1,3]{2,1,0:T(1,128)S(1)}, u32[]{:S(2)}, u32[]{:S(2)}) async-start(s32[4,1,3]{2,1,0:T(1,128)} %bitcast.5), calls=%async_computation | async-start | bytes 4096 | tf_op jit(solution)/shard_map/all_to_all | solution.py:121
  14.2 4.6 %copy-start.1 = (bf16[896,2048]{1,0:T(8,128)(2,1)S(1)}, bf16[896,2048]{1,0:T(8,128)(2,1)}, u32[]{:S(2)}) copy-start(bf16[896,2048]{1,0:T(8,128)(2,1)} %param.13) | copy-start | bytes 11010052
  18.8 9.1 %copy-start.7 = (s32[4]{0:T(128)S(1)}, s32[4]{0:T(128)}, u32[]{:S(2)}) copy-start(s32[4]{0:T(128)} %constant.147) | copy-start | bytes 52
  21.7 12.3 %all-to-all-start.2 = ((s32[8,1,8]{2,1,0:T(1,128)}), s32[8,1,8]{2,1,0:T(1,128)S(1)}, u32[]{:S(2)}, u32[]{:S(2)}) async-start(s32[8,1,8]{2,1,0:T(1,128)} %broadcast_in_dim.53), calls=%async_computation.2 | async-start | bytes 8192 | tf_op jit(solution)/shard_map/all_to_all | solution.py:126
  34.0 5.0 %copy-start.6 = (s32[1,4,2]{1,2,0:T(2,128)S(1)}, s32[1,4,2]{1,2,0:T(2,128)}, u32[]{:S(2)}) copy-start(s32[1,4,2]{1,2,0:T(2,128)} %param.15) | copy-start | bytes 100
  34.0 5.2 %copy-start.5 = (bf16[1,256,2048]{2,1,0:T(8,128)(2,1)S(1)}, bf16[1,256,2048]{2,1,0:T(8,128)(2,1)}, u32[]{:S(2)}) copy-start(bf16[1,256,2048]{2,1,0:T(8,128)(2,1)} %param.10) | copy-start | bytes 3145732
  34.0 37.6 %all-to-all-start.1 = ((bf16[4,3,128,896]{3,2,1,0:T(8,128)(2,1)}), bf16[4,3,128,896]{3,2,1,0:T(8,128)(2,1)}, u32[]{:S(2)}, u32[]{:S(2)}) async-start(bf16[4,3,128,896]{3,2,1,0:T(8,128)(2,1)} %broadcast_select_fusion), calls=%async_computation.1 | async-start | bytes 5505024 | tf_op jit(solution)/shard_map/all_to_all | solution.py:123
  77.2 14.0 %copy-start.8 = (s32[896]{0:T(1024)S(1)}, s32[896]{0:T(1024)}, u32[]{:S(2)}) copy-start(s32[896]{0:T(1024)} %constant.139.clone) | copy-start | bytes 10756
  129.6 7.6 %copy-start.4 = (bf16[896,2048]{1,0:T(8,128)(2,1)}, bf16[896,2048]{1,0:T(8,128)(2,1)S(1)}, u32[]{:S(2)}) copy-start(bf16[896,2048]{1,0:T(8,128)(2,1)S(1)} %fusion.4) | copy-start | bytes 11010052
  134.2 4.7 %copy-start.2 = (bf16[896,2048]{1,0:T(8,128)(2,1)}, bf16[896,2048]{1,0:T(8,128)(2,1)S(1)}, u32[]{:S(2)}) copy-start(bf16[896,2048]{1,0:T(8,128)(2,1)S(1)} %fusion.7) | copy-start | bytes 11010052
  135.0 28.0 %collective-permute-start.2 = (bf16[63,2048]{1,0:T(8,128)(2,1)}, bf16[63,2048]{1,0:T(8,128)(2,1)}, u32[]{:S(2)}, u32[]{:S(2)}) collective-permute-start(bf16[63,2048]{1,0:T(8,128)(2,1)} %slice.58), channel_id=1, source_target_pairs={{0,1},{1,2},{2,3},{4,5},{5,6},{6,7},{8,9},{9,10},{10,11},{12,13},{... | collective-permute-start | bytes 774152 | tf_op jit(solution)/shard_map/ppermute | solution.py:18
  138.7 26.4 %collective-permute-start.4 = (bf16[448,2048]{1,0:T(8,128)(2,1)}, bf16[448,2048]{1,0:T(8,128)(2,1)}, u32[]{:S(2)}, u32[]{:S(2)}) collective-permute-start(bf16[448,2048]{1,0:T(8,128)(2,1)} %constant_dynamic-slice_fusion.11), channel_id=1, source_target_pairs={{0,1},{1,0},{2,3},{3,2},{4,5},{5,4},{6,7},{7,6},{8,9},{9,8},{10,11... | collective-permute-start | bytes 5505032 | tf_op jit(solution)/shard_map/ppermute | solution.py:79
  140.3 28.0 %collective-permute-start.9 = (bf16[448,2048]{1,0:T(8,128)(2,1)}, bf16[448,2048]{1,0:T(8,128)(2,1)}, u32[]{:S(2)}, u32[]{:S(2)}) collective-permute-start(bf16[448,2048]{1,0:T(8,128)(2,1)} %constant_dynamic-slice_fusion.6), channel_id=1, source_target_pairs={{0,1},{1,0},{2,3},{3,2},{4,5},{5,4},{6,7},{7,6},{8,9},{9,8},{10,11... | collective-permute-start | bytes 5505032 | tf_op jit(solution)/shard_map/ppermute | solution.py:79
  152.8 19.9 %collective-permute-start.3 = (bf16[63,2048]{1,0:T(8,128)(2,1)}, bf16[63,2048]{1,0:T(8,128)(2,1)}, u32[]{:S(2)}, u32[]{:S(2)}) collective-permute-start(bf16[63,2048]{1,0:T(8,128)(2,1)} %slice.60), channel_id=1, source_target_pairs={{0,1},{1,2},{2,3},{4,5},{5,6},{6,7},{8,9},{9,10},{10,11},{12,13},{... | collective-permute-start | bytes 774152 | tf_op jit(solution)/shard_map/ppermute | solution.py:18
  157.0 57.5 %all-to-all-start.3 = ((bf16[8,8,16,896]{3,2,1,0:T(8,128)(2,1)}), bf16[8,8,16,896]{3,2,1,0:T(8,128)(2,1)S(1)}, u32[]{:S(2)}, u32[]{:S(2)}) async-start(bf16[8,8,16,896]{3,2,1,0:T(8,128)(2,1)} %bitcast.55), calls=%async_computation.3 | async-start | bytes 3670016 | tf_op jit(solution)/shard_map/all_to_all | solution.py:163
  165.2 3.2 %copy-start.3 = (bf16[896,2048]{1,0:T(8,128)(2,1)S(1)}, bf16[896,2048]{1,0:T(8,128)(2,1)}, u32[]{:S(2)}) copy-start(bf16[896,2048]{1,0:T(8,128)(2,1)} %copy-done.2) | copy-start | bytes 11010052
  168.3 23.4 %collective-permute-start.5 = (bf16[224,2048]{1,0:T(8,128)(2,1)S(1)}, bf16[224,2048]{1,0:T(8,128)(2,1)S(1)}, u32[]{:S(2)}, u32[]{:S(2)}) collective-permute-start(bf16[224,2048]{1,0:T(8,128)(2,1)S(1)} %constant_dynamic-slice_fusion.10), channel_id=1, source_target_pairs={{0,2},{1,3},{2,0},{3,1},{4,6},{5,7},{6,4},{7,5},{8,10},{9,11},{10,... | collective-permute-start | bytes 2752520 | tf_op jit(solution)/shard_map/ppermute | solution.py:79
  170.7 38.6 %collective-permute-start.10 = (bf16[224,2048]{1,0:T(8,128)(2,1)S(1)}, bf16[224,2048]{1,0:T(8,128)(2,1)S(1)}, u32[]{:S(2)}, u32[]{:S(2)}) collective-permute-start(bf16[224,2048]{1,0:T(8,128)(2,1)S(1)} %constant_dynamic-slice_fusion.5), channel_id=1, source_target_pairs={{0,2},{1,3},{2,0},{3,1},{4,6},{5,7},{6,4},{7,5},{8,10},{9,11},{10,... | collective-permute-start | bytes 2752520 | tf_op jit(solution)/shard_map/ppermute | solution.py:79
  192.0 20.2 %collective-permute-start.6 = (bf16[112,2048]{1,0:T(8,128)(2,1)S(1)}, bf16[112,2048]{1,0:T(8,128)(2,1)S(1)}, u32[]{:S(2)}, u32[]{:S(2)}) collective-permute-start(bf16[112,2048]{1,0:T(8,128)(2,1)S(1)} %constant_dynamic-slice_fusion.9), channel_id=1, source_target_pairs={{0,4},{4,0},{8,12},{12,8},{16,20},{20,16},{24,28},{28,24},{1,5},{5... | collective-permute-start | bytes 1376264 | tf_op jit(solution)/shard_map/ppermute | solution.py:79
  210.4 14.9 %collective-permute-start.11 = (bf16[112,2048]{1,0:T(8,128)(2,1)}, bf16[112,2048]{1,0:T(8,128)(2,1)}, u32[]{:S(2)}, u32[]{:S(2)}) collective-permute-start(bf16[112,2048]{1,0:T(8,128)(2,1)} %constant_dynamic-slice_fusion.4), channel_id=1, source_target_pairs={{0,4},{4,0},{8,12},{12,8},{16,20},{20,16},{24,28},{28,24},{1,5},{5... | collective-permute-start | bytes 1376264 | tf_op jit(solution)/shard_map/ppermute | solution.py:79
  213.0 14.1 %collective-permute-start.7 = (bf16[56,2048]{1,0:T(8,128)(2,1)}, bf16[56,2048]{1,0:T(8,128)(2,1)S(1)}, u32[]{:S(2)}, u32[]{:S(2)}) collective-permute-start(bf16[56,2048]{1,0:T(8,128)(2,1)} %constant_dynamic-slice_fusion.8), channel_id=1, source_target_pairs={{0,8},{4,12},{8,0},{12,4},{16,24},{20,28},{24,16},{28,20},{1,9},{5... | collective-permute-start | bytes 688136 | tf_op jit(solution)/shard_map/ppermute | solution.py:79
  223.4 14.0 %copy-start = (bf16[4,32,16,896]{3,2,1,0:T(8,128)(2,1)S(1)}, bf16[4,32,16,896]{3,2,1,0:T(8,128)(2,1)}, u32[]{:S(2)}) copy-start(bf16[4,32,16,896]{3,2,1,0:T(8,128)(2,1)} %gather_fusion.2) | copy-start | bytes 11010052
  225.2 12.2 %collective-permute-start.14 = (bf16[2,32,16,896]{3,2,1,0:T(8,128)(2,1)S(1)}, bf16[2,32,16,896]{3,2,1,0:T(8,128)(2,1)S(1)}, u32[]{:S(2)}, u32[]{:S(2)}) collective-permute-start(bf16[2,32,16,896]{3,2,1,0:T(8,128)(2,1)S(1)} %constant_dynamic-slice_fusion.1), channel_id=1, source_target_pairs={{0,1},{1,0},{2,3},{3,2},{4,5},{5,4},{6,7},{7,6},{8,9},{9,8},{10,11... | collective-permute-start | bytes 5505032 | tf_op jit(solution)/shard_map/ppermute | solution.py:79
  226.5 10.9 %collective-permute-start.12 = (bf16[56,2048]{1,0:T(8,128)(2,1)S(1)}, bf16[56,2048]{1,0:T(8,128)(2,1)S(1)}, u32[]{:S(2)}, u32[]{:S(2)}) collective-permute-start(bf16[56,2048]{1,0:T(8,128)(2,1)S(1)} %constant_dynamic-slice_fusion.3), channel_id=1, source_target_pairs={{0,8},{4,12},{8,0},{12,4},{16,24},{20,28},{24,16},{28,20},{1,9},{5... | collective-permute-start | bytes 688136 | tf_op jit(solution)/shard_map/ppermute | solution.py:79
  227.3 11.6 %collective-permute-start.8 = (bf16[28,2048]{1,0:T(8,128)(2,1)S(1)}, bf16[28,2048]{1,0:T(8,128)(2,1)S(1)}, u32[]{:S(2)}, u32[]{:S(2)}) collective-permute-start(bf16[28,2048]{1,0:T(8,128)(2,1)S(1)} %constant_dynamic-slice_fusion.7), channel_id=1, source_target_pairs={{0,16},{4,20},{8,24},{12,28},{16,0},{20,4},{24,8},{28,12},{1,17},{... | collective-permute-start | bytes 344072 | tf_op jit(solution)/shard_map/ppermute | solution.py:79
  238.0 22.0 %collective-permute-start.15 = (bf16[1,32,16,896]{3,2,1,0:T(8,128)(2,1)S(1)}, bf16[1,32,16,896]{3,2,1,0:T(8,128)(2,1)S(1)}, u32[]{:S(2)}, u32[]{:S(2)}) collective-permute-start(bf16[1,32,16,896]{3,2,1,0:T(8,128)(2,1)S(1)} %constant_dynamic-slice_fusion), channel_id=1, source_target_pairs={{0,2},{1,3},{2,0},{3,1},{4,6},{5,7},{6,4},{7,5},{8,10},{9,11},{10,... | collective-permute-start | bytes 2752520 | tf_op jit(solution)/shard_map/ppermute | solution.py:79
  238.4 8.2 %collective-permute-start.13 = (bf16[28,2048]{1,0:T(8,128)(2,1)S(1)}, bf16[28,2048]{1,0:T(8,128)(2,1)S(1)}, u32[]{:S(2)}, u32[]{:S(2)}) collective-permute-start(bf16[28,2048]{1,0:T(8,128)(2,1)S(1)} %constant_dynamic-slice_fusion.2), channel_id=1, source_target_pairs={{0,16},{4,20},{8,24},{12,28},{16,0},{20,4},{24,8},{28,12},{1,17},{... | collective-permute-start | bytes 344072 | tf_op jit(solution)/shard_map/ppermute | solution.py:79
where the time goes:
time: 262 us; the launch traced here: 261 us
  waiting for transfers between devices  86.7 us (33%)
  starting transfers between devices  42.4 us (16%)
  local copies, waits for them, and re-layouts  40.2 us (15%)
  matrix products  37.4 us (14%)
  Pallas kernels  31.8 us (12%)
  other arithmetic  21.6 us (8%)
    ppermute x12, waiting for transfers between devices, halve(): got = lax.ppermute(give, axis, [(i, i ^ bit) for i in range(size)])  59.4 us
    dot_general x6, matrix products, dot(): lax.dot_general(a, b, (dims, ((), ())), preferred_element_type=jnp.float32)  37.4 us
    pallas_call x1, Pallas kernels, attend(): pl.pallas_call(functools.partial(attend_kernel, scale), grid=(stretches,)...  31.8 us
    all_to_all x1, waiting for transfers between devices, body(): lax.all_to_all(picked, 'db', split_axis=0, concat_axis=0, tiled=True)  27.3 us
    ppermute x12, starting transfers between devices, halve(): got = lax.ppermute(give, axis, [(i, i ^ bit) for i in range(size)])  11.8 us
    unnamed x23, local copies, waits for them, and re-layouts  9.12 us
    convert_element_type x9, other arithmetic, halve_all(): block = halve(block, axis, bit).astype(jnp.bfloat16)  7.69 us
    ppermute x4, starting transfers between devices, from_behind(): return lax.ppermute(block, axis, route)  7.53 us
  transfers between devices with their start and end apart: 20, of which 6 were waited for; matrix products, arithmetic and copies ran while one was open for 25% of the time, Pallas kernels for 0%

commit v1 on v0

--- a/solution.py
+++ b/solution.py
@@ -96,6 +96,224 @@
     return np.array([int(format(i, "b").zfill(bits)[::-1], 2) if bits else 0 for i in range(count)])
 
 
+def finish_kernel(
+    piece, lt_any, both_any, w_any, member_any, spread_ref,
+    gk_ref, gv_ref, gd_ref,
+    lt, both, wts, member, grad, got1, got2, got3, zed, got4, got5,
+    dsend, arrived, give, dgot1, mine, xgive, dgot2,
+    load_sem, send_sem, recv_sem, asend_sem, arecv_sem,
+):
+    bf, f32 = jnp.bfloat16, jnp.float32
+    mesh_ids = pl.DeviceIdType.MESH
+    dp, db = lax.axis_index("dp"), lax.axis_index("db")
+    seqs = arrived.shape[0]
+    c, x = lax.rem(db, 2), db // 2
+    y, z0, z1 = lax.rem(dp, 2), lax.rem(dp // 2, 2), dp // 4
+    pc = (dp, db + 1 - 2 * c)
+    px = (dp, db + 2 - 4 * x)
+    py = (dp + 1 - 2 * y, db)
+    pz0 = (dp + 2 - 4 * z0, db)
+    pz1 = (dp + 4 - 8 * z1, db)
+    others = [(lax.rem(dp + d, seqs), db) for d in range(1, seqs)]
+    loads = [
+        pltpu.make_async_copy(lt_any, lt, load_sem.at[0]),
+        pltpu.make_async_copy(both_any, both, load_sem.at[1]),
+        pltpu.make_async_copy(w_any, wts, load_sem.at[2]),
+        pltpu.make_async_copy(member_any, member, load_sem.at[3]),
+    ]
+    for load in loads:
+        load.start()
+    barrier = pltpu.get_barrier_semaphore()
+    for peer in [pc, px] + others:
+        pl.semaphore_signal(barrier, inc=1, device_id=peer, device_id_type=mesh_ids)
+    pl.semaphore_wait(barrier, 2 + len(others))
+    copies = []
+
+    def send(src, dst, peer, sems=None):
+        number = len(copies)
+        copy = pltpu.make_async_remote_copy(
+            src_ref=src,
+            dst_ref=dst,
+            send_sem=send_sem.at[number] if sems is None else asend_sem.at[sems],
+            recv_sem=recv_sem.at[number] if sems is None else arecv_sem.at[sems],
+            device_id=peer,
+            device_id_type=mesh_ids,
+        )
+        copy.start()
+        if sems is None:
+            copies.append(copy)
+        return copy
+
+    def add(a, b):
+        return (a.astype(f32) + b.astype(f32)).astype(bf)
+
+    half = both.shape[1] // 2
+    quarter = grad.shape[4]
+    tile = 512
+
+    def weight_grad(p):
+        @pl.loop(0, half // tile)
+        def _(t):
+            cols = pl.ds(pl.multiple_of(p * half + t * tile, tile), tile)
+            into = pl.ds(pl.multiple_of(t * tile, tile), tile)
+            out = jnp.dot(lt[...], both[:, cols], preferred_element_type=f32).astype(bf)
+            for b in range(8):
+                grad[p, b // 4, b // 2 % 2, b % 2, :, into] = out[b * quarter : (b + 1) * quarter]
+
+        return send(grad.at[p, 1 - c], got1.at[p], pc)
+
+    def after_core(p, copy):
+        copy.wait_recv()
+        for i in range(2):
+            for j in range(2):
+                grad[p, c, i, j] = add(grad[p, c, i, j], got1[p, i, j])
+
+    asked = dsend.shape[2] // piece
+    rows = both.shape[0] // 2
+
+    def states_grad(h):
+        out = lax.dot_general(
+            both[h * rows : (h + 1) * rows], wts[...], (((1,), (1,)), ((), ())),
+            preferred_element_type=f32,
+        ).astype(bf)
+        for r in range(asked):
+            for j in range(seqs):
+                start = (r * seqs + j) * piece
+                dsend[h, j, r * piece : (r + 1) * piece] = out[start : start + piece]
+        arrived[dp, h] = dsend[h, dp]
+        return [
+            send(dsend.at[h, peer[0]], arrived.at[dp, h], peer, (h, d))
+            for d, peer in enumerate(others)
+        ]
+
+    loads[0].wait()
+    loads[1].wait()
+    key1 = weight_grad(0)
+    loads[2].wait()
+    across = states_grad(0)
+    after_core(0, key1)
+    key2 = send(grad.at[0, c, 1 - x], got2.at[0], px)
+    across += states_grad(1)
+    value1 = weight_grad(1)
+    after_core(1, value1)
+    value2 = send(grad.at[1, c, :, 1 - y], got2.at[1], py)
+
+    def expand(p, total):
+        zed[p] = (
+            jnp.dot(spread_ref[...], total, preferred_element_type=f32)
+            .astype(bf)
+            .reshape(zed.shape[1:])
+        )
+        return send(zed.at[p, 1 - z0], got4.at[p], pz0)
+
+    key2.wait_recv()
+    for j in range(2):
+        grad[0, c, x, j] = add(grad[0, c, x, j], got2[0, j])
+    key3 = send(grad.at[0, c, x, 1 - y], got3.at[0], py)
+    value2.wait_recv()
+    for i in range(2):
+        grad[1, c, i, y] = add(grad[1, c, i, y], got2[1, i])
+    value3 = send(grad.at[1, c, 1 - x, y], got3.at[1], px)
+    key3.wait_recv()
+    key4 = expand(0, add(grad[0, c, x, y], got3[0]))
+    value3.wait_recv()
+    value4 = expand(1, add(grad[1, c, x, y], got3[1]))
+
+    for copy in across:
+        copy.wait_recv()
+    loads[3].wait()
+    block = gd_ref.shape[0]
+    every = arrived.shape[0] * arrived.shape[1] * arrived.shape[2]
+
+    def dense(shard):
+        return jnp.dot(
+            member[pl.ds(pl.multiple_of(shard * block, block), block)],
+            arrived[...].reshape(every, arrived.shape[3]),
+            preferred_element_type=f32,
+        )
+
+    core = []
+    for far in (1, 0):
+        side = x if far == 0 else 1 - x
+        give[far] = dense(2 * side + 1 - c).astype(bf)
+        core.append(send(give.at[far], dgot1.at[far], pc))
+    for far in (1, 0):
+        side = x if far == 0 else 1 - x
+        mine[far] = dense(2 * side + c)
+    core[0].wait_recv()
+    xgive[...] = (mine[1] + dgot1[1].astype(f32)).astype(bf)
+    xcopy = send(xgive, dgot2, px)
+
+    def last(p, copy):
+        copy.wait_recv()
+        for j in range(2):
+            zed[p, z0, j] = add(zed[p, z0, j], got4[p, j])
+        return send(zed.at[p, z0, 1 - z1], got5.at[p], pz1)
+
+    key5 = last(0, key4)
+    value5 = last(1, value4)
+    core[1].wait_recv()
+    mine[0] = mine[0] + dgot1[0].astype(f32)
+    for p, copy, out_ref in ((0, key5, gk_ref), (1, value5, gv_ref)):
+        copy.wait_recv()
+        total = zed[p, z0, z1].astype(f32) + got5[p].astype(f32)
+        out_ref[...] = total[: out_ref.shape[0]]
+    xcopy.wait_recv()
+    gd_ref[...] = (mine[0] + dgot2[...].astype(f32)).astype(bf)
+    for copy in copies + across:
+        copy.wait_send()
+
+
+def finish(lt, both, w_both, member, spread, share, seqs, block, piece):
+    enc, rows = lt.shape
+    wide = both.shape[1]
+    half = wide // 2
+    quarter = enc // 8
+    padded = spread.shape[0] // 4
+    bf = jnp.bfloat16
+    own = member.shape[1] // seqs
+    anywhere = pl.BlockSpec(memory_space=pl.ANY)
+    vmem = pl.BlockSpec(memory_space=pltpu.VMEM)
+    return pl.pallas_call(
+        functools.partial(finish_kernel, piece),
+        in_specs=[anywhere] * 4 + [vmem],
+        out_specs=[vmem] * 3,
+        out_shape=[
+            jax.ShapeDtypeStruct((share, half), jnp.float32),
+            jax.ShapeDtypeStruct((share, half), jnp.float32),
+            jax.ShapeDtypeStruct((block, enc), bf),
+        ],
+        scratch_shapes=[
+            pltpu.VMEM(lt.shape, bf),
+            pltpu.VMEM(both.shape, bf),
+            pltpu.VMEM(w_both.shape, bf),
+            pltpu.VMEM(member.shape, bf),
+            pltpu.VMEM((2, 2, 2, 2, quarter, half), bf),
+            pltpu.VMEM((2, 2, 2, quarter, half), bf),
+            pltpu.VMEM((2, 2, quarter, half), bf),
+            pltpu.VMEM((2, quarter, half), bf),
+            pltpu.VMEM((2, 2, 2, padded, half), bf),
+            pltpu.VMEM((2, 2, padded, half), bf),
+            pltpu.VMEM((2, padded, half), bf),
+            pltpu.VMEM((2, seqs, own // 2, enc), bf),
+            pltpu.VMEM((seqs, 2, own // 2, enc), bf),
+            pltpu.VMEM((2, block, enc), bf),
+            pltpu.VMEM((2, block, enc), bf),
+            pltpu.VMEM((2, block, enc), jnp.float32),
+            pltpu.VMEM((block, enc), bf),
+            pltpu.VMEM((block, enc), bf),
+            pltpu.SemaphoreType.DMA((4,)),
+            pltpu.SemaphoreType.DMA((16,)),
+            pltpu.SemaphoreType.DMA((16,)),
+            pltpu.SemaphoreType.DMA((2, seqs - 1)),
+            pltpu.SemaphoreType.DMA((2, seqs - 1)),
+        ],
+        compiler_params=pltpu.CompilerParams(
+            vmem_limit_bytes=62 << 20, collective_id=0, has_side_effects=True
+        ),
+    )(lt, both, w_both, member, spread)
+
+
 def body(queries, cotangent, w_key, w_value, database, nb_shard, nb_row):
     q_local = queries[0]
     g_local = cotangent[0]
@@ -119,19 +337,18 @@
     )
     send_ids = jnp.sum(place * wanted[:, None], axis=0).reshape(shards, slot_count)
     asked = lax.all_to_all(send_ids, "db", split_axis=0, concat_axis=0, tiled=True)
-    picked = jnp.take(database, asked, axis=0)
-    returned = lax.all_to_all(picked, "db", split_axis=0, concat_axis=0, tiled=True)
-
+    picked = jnp.take(database, asked, axis=0, mode="clip")
+    held, w_key, w_value, target, wanted = lax.optimization_barrier(
+        (picked, w_key, w_value, target, wanted)
+    )
     ids = jnp.broadcast_to((target * db_count + wanted)[None], (seqs, asks))
     ids = lax.all_to_all(ids, "dp", split_axis=0, concat_axis=0, tiled=True).reshape(seqs * asks)
-    member = (
-        ids[None, :] == jnp.arange(shards * db_count, dtype=jnp.int32)[:, None]
-    ).astype(jnp.bfloat16)
+    w_both = jnp.concatenate([w_key, w_value], axis=1)
+    returned = lax.all_to_all(held, "db", split_axis=0, concat_axis=0, tiled=True)
 
     next_q, next_g = from_behind((q_local[:span], g_local[:span]), "db", -1)
     block_q = jnp.concatenate([q_local[span - 1 :], next_q[: span - 1]], axis=0)
     block_g = jnp.concatenate([g_local[span - 1 :], next_g[: span - 1]], axis=0)
-    w_both = jnp.concatenate([w_key, w_value], axis=1)
 
     devices = shards * seqs
     share = enc_width // devices
@@ -139,26 +356,50 @@
     shuffle = (
         jnp.arange(enc_width, dtype=jnp.int32)[:, None] == jnp.asarray(source, jnp.int32)[None, :]
     ).astype(jnp.bfloat16)
-
-    states = jnp.take(returned.reshape(shards * slot_count, nb_len, enc_width), slot_pos, axis=0)
+    piece = nb_len // seqs
+    fused = shards == 4 and seqs == 8
+    if fused:
+        row = jnp.arange(shards * db_count * piece, dtype=jnp.int32)[:, None]
+        col = jnp.arange(seqs * asks * piece, dtype=jnp.int32)[None, :]
+        member = (
+            (jnp.broadcast_to(ids[:, None], (seqs * asks, piece)).reshape(1, -1) == row // piece) & (row % piece == col % piece)
+        ).astype(jnp.bfloat16)
+        padded = -(-share // 16) * 16
+        row = jnp.arange(4 * padded, dtype=jnp.int32)[:, None]
+        col = jnp.arange(4 * share, dtype=jnp.int32)[None, :]
+        spread = ((row // padded == col // share) & (row % padded == col % share)).astype(
+            jnp.bfloat16
+        )
+    else:
+        member = (
+            ids[None, :] == jnp.arange(shards * db_count, dtype=jnp.int32)[:, None]
+        ).astype(jnp.bfloat16)
+
+    states = jnp.take(returned.reshape(shards * slot_count, nb_len, enc_width), slot_pos, axis=0, mode="clip")
     states = states.reshape(asks * nb_len, enc_width)
     kv = dot(states, w_both, ((1,), (0,))).astype(jnp.bfloat16)
+    outputs, dquery, both = attend(block_q, block_g, kv, stretch_count)
+
+    keep = rows_local - span + 1
+    prev_out, prev_dq = from_behind((outputs[keep:], dquery[keep:]), "db", 1)
+    attn_out = jnp.concatenate([prev_out, outputs[:keep]], axis=0)[None]
+    grad_queries = jnp.concatenate([prev_dq, dquery[:keep]], axis=0)[None]
+
+    if fused:
+        shuffled = dot(shuffle, states, ((0,), (1,))).astype(jnp.bfloat16)
+        *grads, grad_database = finish(
+            shuffled, both, w_both, member, spread, share, seqs, db_count * piece, piece
+        )
+        grad_database = grad_database.reshape(db_count, piece, enc_width)
+        return (attn_out, grad_queries, grads[0], grads[1], grad_database)
+
     shuffled = dot(states, shuffle, ((1,), (0,))).astype(jnp.bfloat16)
-    outputs, dquery, both = attend(block_q, block_g, kv, stretch_count)
-
     steps = [("db", b) for b in bits_of("db")] + [("dp", b) for b in bits_of("dp")]
     grads = []
     for part in range(2):
         grad = dot(shuffled, both[:, part * width : (part + 1) * width], ((0,), (0,)))
         grads.append(halve_all(grad.astype(jnp.bfloat16), steps))
-
-    keep = rows_local - span + 1
-    prev_out, prev_dq = from_behind((outputs[keep:], dquery[keep:]), "db", 1)
-    attn_out = jnp.concatenate([prev_out, outputs[:keep]], axis=0)[None]
-    grad_queries = jnp.concatenate([prev_dq, dquery[:keep]], axis=0)[None]
-
     dstates = dot(both, w_both, ((1,), (1,))).astype(jnp.bfloat16)
-    piece = nb_len // seqs
     dstates = dstates.reshape(asks, seqs, piece, enc_width).transpose(1, 0, 2, 3)
     arrived = lax.all_to_all(dstates, "dp", split_axis=0, concat_axis=0, tiled=True)
     dense = dot(member, arrived.reshape(seqs * asks, piece * enc_width), ((1,), (0,)))

time: 262 us -> 237 us (0.905)
  Pallas kernels: 31.8 us -> 128 us
  waiting for transfers between devices: 86.7 us -> 27 us
  matrix products: 37.4 us -> 17.1 us
  starting transfers between devices: 42.4 us -> 22.3 us
  local copies, waits for them, and re-layouts: 40.2 us -> 27.4 us
  other arithmetic: 21.6 us -> 12.3 us
    pallas_call x0 -> x1, Pallas kernels: none -> 96.1 us  [finish(): pl.pallas_call(functools.partial(finish_kernel, piece), in_specs=[anywher...]
    ppermute x12 -> x0, waiting for transfers between devices: 59.4 us -> none  [halve(): got = lax.ppermute(give, axis, [(i, i ^ bit) for i in range(size)])]
    dot_general x6 -> x2, matrix products: 37.4 us -> 17.1 us  [dot(): lax.dot_general(a, b, (dims, ((), ())), preferred_element_type=jnp.float32)]
    ppermute x12 -> x0, starting transfers between devices: 11.8 us -> none  [halve(): got = lax.ppermute(give, axis, [(i, i ^ bit) for i in range(size)])]
    dynamic_slice x12 -> x0, local copies, waits for them, and re-layouts: 6.67 us -> none  [halve(): give = lax.dynamic_slice_in_dim(block, (1 - side) * half, half, 0)]
    all_to_all x2 -> x1, waiting for transfers between devices: 27.3 us -> 20.7 us  [body(): lax.all_to_all(held, 'db', split_axis=0, concat_axis=0, tiled=True)]
    all_to_all x1, waiting for transfers between devices: 0.01 us -> 6.37 us  [body(): lax.all_to_all(ids, 'dp', split_axis=0, concat_axis=0, tiled=True)]
    all_to_all x2 -> x1, starting transfers between devices: 10.9 us -> 4.64 us  [body(): lax.all_to_all(held, 'db', split_axis=0, concat_axis=0, tiled=True)]
  transfers between devices with their start and end apart: 20 -> 7, of which waited for: 6 -> 2; matrix products, arithmetic and copies ran while one was open for 25% -> 13% of each run, Pallas kernels for 0% -> 41%
where the time goes in v1:
time: 237 us; the launch traced here: 235 us
  Pallas kernels  128 us (54%)
  local copies, waits for them, and re-layouts  27.4 us (12%)
  waiting for transfers between devices  27 us (11%)
  starting transfers between devices  22.3 us (9%)
  matrix products  17.1 us (7%)
  other arithmetic  12.3 us (5%)
    pallas_call x1, Pallas kernels, finish(): pl.pallas_call(functools.partial(finish_kernel, piece), in_specs=[anywher...  96.1 us
    pallas_call x1, Pallas kernels, attend(): pl.pallas_call(functools.partial(attend_kernel, scale), grid=(stretches,)...  32 us
    all_to_all x1, waiting for transfers between devices, body(): lax.all_to_all(held, 'db', split_axis=0, concat_axis=0, tiled=True)  20.7 us
    dot_general x2, matrix products, dot(): lax.dot_general(a, b, (dims, ((), ())), preferred_element_type=jnp.float32)  17.1 us
    unnamed x22, local copies, waits for them, and re-layouts  8.5 us
    ppermute x4, starting transfers between devices, from_behind(): return lax.ppermute(block, axis, route)  7.1 us
    all_to_all x1, waiting for transfers between devices, body(): lax.all_to_all(ids, 'dp', split_axis=0, concat_axis=0, tiled=True)  6.37 us
    all_to_all x1, starting transfers between devices, body(): lax.all_to_all(ids, 'dp', split_axis=0, concat_axis=0, tiled=True)  6.31 us
  transfers between devices with their start and end apart: 7, of which 2 were waited for; matrix products, arithmetic and copies ran while one was open for 13% of the time, Pallas kernels for 41%

profile of v1, /device:TPU:0, one launch (start us, length us, event | category | flops | bytes accessed | tf_op | source)
XLA Modules:
  0.0 235.0 jit_solution(9905647570155104518)
XLA Ops:
  0.6 0.8 copy.23
  1.4 0.1 reshape_squeeze.4
  1.5 0.2 reduce_window_sum.11
  1.7 0.8 copy.24
  2.5 0.1 mul.34
  2.6 0.1 select_reduce_fusion
  2.6 0.7 all_to_all.13
  3.3 4.2 %all-to-all-start = ((s32[4,1,3]{2,1,0:T(1,128)}), s32[4,1,3]{2,1,0:T(1,128)S(1)}, u32[]{:S(2)}, u32[]{:S(2)}) async-start(s32[4,1,3]{2,1,0:T(1,128)} %bitcast.4), calls=%async_computation | async-start | bytes 4096 | tf_op jit(solution)/shard_map/all_to_all | solution.py:339
  7.5 1.0 slice_bitcast_fusion.3
  8.5 1.3 collective-permute-start
  9.8 1.0 slice_bitcast_fusion.2
  10.8 1.3 collective-permute-start.1
  12.1 0.7 broadcast_multiply_fusion
  12.7 1.3 slice_bitcast_fusion.1
  14.1 0.1 copy.26
  14.2 0.1 mul.38
  14.3 0.7 and_convert_fusion.1.spread_ref
  15.0 0.0 all-to-all-done
  15.0 0.5 broadcast.245
  15.6 0.7 reduce.6
  16.2 0.1 reshape.220
  16.3 5.7 %gather_fusion = bf16[12,128,896]{2,1,0:T(8,128)(2,1)} fusion(bf16[32,128,896]{2,1,0:T(8,128)(2,1)} %param.12, s32[1024]{0:T(1024)S(1)} %pad_clamp_fusion.1), kind=kCustom, calls=%fused_computation | custom fusion | bytes 5505072 | tf_op jit(solution)/shard_map/jit(_take)/gather | solution.py:340
  22.0 0.6 broadcast_in_dim.18
  22.6 6.3 %all-to-all-start.2 = ((s32[8,1,8]{2,1,0:T(1,128)}), s32[8,1,8]{2,1,0:T(1,128)S(1)}, u32[]{:S(2)}, u32[]{:S(2)}) async-start(s32[8,1,8]{2,1,0:T(1,128)} %broadcast_in_dim.18), calls=%async_computation.2 | async-start | bytes 8192 | tf_op jit(solution)/shard_map/all_to_all | solution.py:345
  29.0 0.0 copy-start.3
  29.0 6.4 %all-to-all-done.2 = s32[8,1,8]{2,1,0:T(1,128)S(1)} async-done(((s32[8,1,8]{2,1,0:T(1,128)}), s32[8,1,8]{2,1,0:T(1,128)S(1)}, u32[]{:S(2)}, u32[]{:S(2)}) %all-to-all-start.2) | async-done | bytes 288 | tf_op jit(solution)/shard_map/all_to_all | solution.py:345
  35.3 4.6 %all-to-all-start.1 = ((bf16[4,3,128,896]{3,2,1,0:T(8,128)(2,1)}), bf16[4,3,128,896]{3,2,1,0:T(8,128)(2,1)}, u32[]{:S(2)}, u32[]{:S(2)}) async-start(bf16[4,3,128,896]{3,2,1,0:T(8,128)(2,1)} %bitcast.5), calls=%async_computation.1 | async-start | bytes 5505024 | tf_op jit(solution)/shard_map/all_to_all | solution.py:347
  40.0 0.0 copy-done.3
  40.0 0.2 slice_bitcast_fusion
  40.2 0.0 copy-start.1
  40.2 4.6 %constant_dynamic-update-slice_fusion.1 = bf16[896,4096]{1,0:T(8,128)(2,1)} fusion(bf16[896,2048]{1,0:T(8,128)(2,1)} %param.10), kind=kLoop, calls=%fused_computation.32 | loop fusion | bytes 7340032
  44.8 0.0 copy-done.1
  44.8 2.4 %constant_dynamic-update-slice_fusion.w_any = bf16[896,4096]{1,0:T(8,128)(2,1)} fusion(bf16[896,4096]{1,0:T(8,128)(2,1)} %constant_dynamic-update-slice_fusion.1, bf16[896,2048]{1,0:T(8,128)(2,1)S(1)} %copy-done.1), kind=kLoop, calls=%fused_computation.31 | loop fusion | bytes 7340032 | tf_op jit(solution)/shard_map/concatenate | solution.py:346
  47.2 0.7 reduce.7
  47.8 0.1 broadcast_in_dim.20
  47.9 0.1 broadcast_in_dim.21
  48.0 0.1 eq.110
  48.1 2.7 %and_convert_fusion.member_any = bf16[2048,1024]{1,0:T(8,128)(2,1)} fusion(s32[1024]{0:T(1024)S(1)} %add_select_fusion.1, s32[1024]{0:T(1024)S(1)} %eq.110, s32[2048]{0:T(1024)S(1)} %get-tuple-element.27, s32[2048]{0:T(1024)S(1)} %get-tuple-element.28), kind=kLoop, calls=%fused_computation.2 | loop fusion | flops 8388608 | bytes 4218880 | tf_op jit(solution)/shard_map/convert_element_type | solution.py:366
  50.8 0.0 collective-permute-done
  50.8 1.1 pad_maximum_fusion.q_ref
  51.9 0.0 collective-permute-done.1
  51.9 1.1 pad_maximum_fusion.1.g_ref
  53.0 20.7 %all-to-all-done.1 = bf16[4,3,128,896]{3,2,1,0:T(8,128)(2,1)} async-done(((bf16[4,3,128,896]{3,2,1,0:T(8,128)(2,1)}), bf16[4,3,128,896]{3,2,1,0:T(8,128)(2,1)}, u32[]{:S(2)}, u32[]{:S(2)}) %all-to-all-start.1) | async-done | bytes 2752544 | tf_op jit(solution)/shard_map/all_to_all | solution.py:347
  73.7 3.8 %gather_fusion.1 = bf16[8,128,896]{2,1,0:T(8,128)(2,1)} fusion(bf16[12,128,896]{2,1,0:T(8,128)(2,1)} %bitcast.6, s32[1024]{0:T(1024)S(1)} %pad_clamp_fusion), kind=kCustom, calls=%fused_computation.1 | custom fusion | bytes 3670048 | tf_op jit(solution)/shard_map/jit(_take)/gather | solution.py:378
  77.5 13.7 %convolution_convert_fusion.kv_ref = bf16[1024,4096]{1,0:T(8,128)(2,1)} fusion(bf16[1024,896]{1,0:T(8,128)(2,1)} %bitcast.28, bf16[896,4096]{1,0:T(8,128)(2,1)} %constant_dynamic-update-slice_fusion.w_any), kind=kOutput, calls=%fused_computation.3 | convolution fusion | flops 7520387072 | bytes 17563648 | tf_op jit(solution)/shard_map/dot_general | solution.py:22
  91.1 32.0 %shard_map.119 = (bf16[256,2048]{1,0:T(8,128)(2,1)S(1)}, bf16[256,2048]{1,0:T(8,128)(2,1)S(1)}, bf16[1024,4096]{1,0:T(8,128)(2,1)S(1)}) custom-call(bf16[256,2048]{1,0:T(8,128)(2,1)S(1)} %pad_maximum_fusion.q_ref, bf16[256,2048]{1,0:T(8,128)(2,1)S(1)} %pad_maximum_fusion.1.g_ref, bf16[1024,4096]{1,0:T(8,128)(2,1)} %convolution_convert_fusion.kv_ref), custom_call_target="tpu_custom_call" | custom-call | flops 1610612736 | bytes 20971520 | tf_op jit(solution)/shard_map/pallas_call | solution.py:54
  123.1 0.0 copy-start
  123.1 0.9 slice.54
  124.0 2.5 %collective-permute-start.3 = (bf16[63,2048]{1,0:T(8,128)(2,1)}, bf16[63,2048]{1,0:T(8,128)(2,1)}, u32[]{:S(2)}, u32[]{:S(2)}) collective-permute-start(bf16[63,2048]{1,0:T(8,128)(2,1)} %slice.54), channel_id=1, source_target_pairs={{0,1},{1,2},{2,3},{4,5},{5,6},{6,7},{8,9},{9,10},{10,11},{12,13},{... | collective-permute-start | bytes 774152 | tf_op jit(solution)/shard_map/ppermute | solution.py:18
  126.5 0.1 slice.52
  126.6 2.0 collective-permute-start.2
  128.6 0.0 copy-done.2
  128.6 0.0 copy-done.7
  128.6 3.4 %convolution_convert_fusion.1.lt_any = bf16[896,1024]{1,0:T(8,128)(2,1)} fusion(bf16[1024,896]{1,0:T(8,128)(2,1)S(1)} %bitcast.29, s32[896]{0:T(1024)S(1)} %copy-done.7), kind=kOutput, calls=%fused_computation.6 | convolution fusion | flops 1646690304 | bytes 3673600 | tf_op jit(solution)/shard_map/dot_general | solution.py:22
  132.0 0.1 slice.55
  132.1 0.1 slice.53
  132.1 96.1 %shard_map.120 = (f32[28,2048]{1,0:T(8,128)}, f32[28,2048]{1,0:T(8,128)}, bf16[512,896]{1,0:T(8,128)(2,1)}) custom-call(bf16[896,1024]{1,0:T(8,128)(2,1)} %convolution_convert_fusion.1.lt_any, bf16[1024,4096]{1,0:T(8,128)(2,1)} %copy-done, bf16[896,4096]{1,0:T(8,128)(2,1)} %constant_dynamic-update-slice_fusion.w_any, ...), custom_call_target="tpu_custom_call" | custom-call | tf_op jit(solution)/shard_map/pallas_call | solution.py:277
  228.3 0.0 collective-permute-done.3
  228.3 2.2 maximum_bitcast_fusion.1
  230.6 0.0 collective-permute-done.2
  230.6 2.1 maximum_bitcast_fusion
  232.7 0.7 copy.31
  233.4 0.7 copy.32
  234.1 0.9 copy.33
  (20 shorter events, 0.1 us)
Async XLA Ops:
  3.3 11.7 %all-to-all-start = ((s32[4,1,3]{2,1,0:T(1,128)}), s32[4,1,3]{2,1,0:T(1,128)S(1)}, u32[]{:S(2)}, u32[]{:S(2)}) async-start(s32[4,1,3]{2,1,0:T(1,128)} %bitcast.4), calls=%async_computation | async-start | bytes 4096 | tf_op jit(solution)/shard_map/all_to_all | solution.py:339
  8.5 42.3 %collective-permute-start = (bf16[64,2048]{1,0:T(8,128)(2,1)S(1)}, bf16[64,2048]{1,0:T(8,128)(2,1)}, u32[]{:S(2)}, u32[]{:S(2)}) collective-permute-start(bf16[64,2048]{1,0:T(8,128)(2,1)S(1)} %slice_bitcast_fusion.3), channel_id=1, source_target_pairs={{1,0},{2,1},{3,2},{5,4},{6,5},{7,6},{9,8},{10,9},{11,10},{13,12},{... | collective-permute-start | bytes 786440 | tf_op jit(solution)/shard_map/ppermute | solution.py:18
  10.8 41.1 %collective-permute-start.1 = (bf16[64,2048]{1,0:T(8,128)(2,1)S(1)}, bf16[64,2048]{1,0:T(8,128)(2,1)}, u32[]{:S(2)}, u32[]{:S(2)}) collective-permute-start(bf16[64,2048]{1,0:T(8,128)(2,1)S(1)} %slice_bitcast_fusion.2), channel_id=1, source_target_pairs={{1,0},{2,1},{3,2},{5,4},{6,5},{7,6},{9,8},{10,9},{11,10},{13,12},{... | collective-permute-start | bytes 786440 | tf_op jit(solution)/shard_map/ppermute | solution.py:18
  22.6 12.7 %all-to-all-start.2 = ((s32[8,1,8]{2,1,0:T(1,128)}), s32[8,1,8]{2,1,0:T(1,128)S(1)}, u32[]{:S(2)}, u32[]{:S(2)}) async-start(s32[8,1,8]{2,1,0:T(1,128)} %broadcast_in_dim.18), calls=%async_computation.2 | async-start | bytes 8192 | tf_op jit(solution)/shard_map/all_to_all | solution.py:345
  29.0 11.0 %copy-start.3 = (bf16[1,256,2048]{2,1,0:T(8,128)(2,1)S(1)}, bf16[1,256,2048]{2,1,0:T(8,128)(2,1)}, u32[]{:S(2)}) copy-start(bf16[1,256,2048]{2,1,0:T(8,128)(2,1)} %param.9) | copy-start | bytes 3145732
  35.3 38.3 %all-to-all-start.1 = ((bf16[4,3,128,896]{3,2,1,0:T(8,128)(2,1)}), bf16[4,3,128,896]{3,2,1,0:T(8,128)(2,1)}, u32[]{:S(2)}, u32[]{:S(2)}) async-start(bf16[4,3,128,896]{3,2,1,0:T(8,128)(2,1)} %bitcast.5), calls=%async_computation.1 | async-start | bytes 5505024 | tf_op jit(solution)/shard_map/all_to_all | solution.py:347
  40.2 4.6 %copy-start.1 = (bf16[896,2048]{1,0:T(8,128)(2,1)S(1)}, bf16[896,2048]{1,0:T(8,128)(2,1)}, u32[]{:S(2)}) copy-start(bf16[896,2048]{1,0:T(8,128)(2,1)} %param.11) | copy-start | bytes 11010052
  91.1 37.5 %copy-start.2 = (bf16[8,128,896]{2,1,0:T(8,128)(2,1)S(1)}, bf16[8,128,896]{2,1,0:T(8,128)(2,1)}, u32[]{:S(2)}) copy-start(bf16[8,128,896]{2,1,0:T(8,128)(2,1)} %gather_fusion.1) | copy-start | bytes 5505028
  91.1 37.5 %copy-start.7 = (s32[896]{0:T(1024)S(1)}, s32[896]{0:T(1024)}, u32[]{:S(2)}) copy-start(s32[896]{0:T(1024)} %constant.96.clone) | copy-start | bytes 10756
  123.1 8.9 %copy-start = (bf16[1024,4096]{1,0:T(8,128)(2,1)}, bf16[1024,4096]{1,0:T(8,128)(2,1)S(1)}, u32[]{:S(2)}) copy-start(bf16[1024,4096]{1,0:T(8,128)(2,1)S(1)} %get-tuple-element.21.both_any) | copy-start | bytes 25165828
  124.0 104.3 %collective-permute-start.3 = (bf16[63,2048]{1,0:T(8,128)(2,1)}, bf16[63,2048]{1,0:T(8,128)(2,1)}, u32[]{:S(2)}, u32[]{:S(2)}) collective-permute-start(bf16[63,2048]{1,0:T(8,128)(2,1)} %slice.54), channel_id=1, source_target_pairs={{0,1},{1,2},{2,3},{4,5},{5,6},{6,7},{8,9},{9,10},{10,11},{12,13},{... | collective-permute-start | bytes 774152 | tf_op jit(solution)/shard_map/ppermute | solution.py:18
  126.6 104.0 %collective-permute-start.2 = (bf16[63,2048]{1,0:T(8,128)(2,1)S(1)}, bf16[63,2048]{1,0:T(8,128)(2,1)}, u32[]{:S(2)}, u32[]{:S(2)}) collective-permute-start(bf16[63,2048]{1,0:T(8,128)(2,1)S(1)} %slice.52), channel_id=1, source_target_pairs={{0,1},{1,2},{2,3},{4,5},{5,6},{6,7},{8,9},{9,10},{10,11},{12,13},{... | collective-permute-start | bytes 774152 | tf_op jit(solution)/shard_map/ppermute | solution.py:18
  228.3 4.4 %copy-start.6 = (f32[28,2048]{1,0:T(8,128)S(1)}, f32[28,2048]{1,0:T(8,128)}, u32[]{:S(2)}) copy-start(f32[28,2048]{1,0:T(8,128)} %get-tuple-element.40) | copy-start | bytes 688132
  228.3 5.1 %copy-start.5 = (f32[28,2048]{1,0:T(8,128)S(1)}, f32[28,2048]{1,0:T(8,128)}, u32[]{:S(2)}) copy-start(f32[28,2048]{1,0:T(8,128)} %get-tuple-element.41) | copy-start | bytes 688132
  228.3 5.8 %copy-start.4 = (bf16[512,896]{1,0:T(8,128)(2,1)S(1)}, bf16[512,896]{1,0:T(8,128)(2,1)}, u32[]{:S(2)}) copy-start(bf16[512,896]{1,0:T(8,128)(2,1)} %get-tuple-element.26) | copy-start | bytes 2752516

commit v2 on v1

--- a/solution.py
+++ b/solution.py
@@ -22,52 +22,77 @@
     return lax.dot_general(a, b, (dims, ((), ())), preferred_element_type=jnp.float32)
 
 
-def attend_kernel(scale, q_ref, g_ref, kv_ref, out_ref, dq_ref, both_ref):
+def attend_kernel(scale, group, slot_ref, q_ref, g_ref, *refs):
+    neigh = len(refs) - 6
+    state_refs, (w_ref, shuffle_ref, out_ref, dq_ref, both_ref, lt_ref) = refs[:neigh], refs[neigh:]
     width = q_ref.shape[1]
-    for head in range(width // HSIZE):
-        cols = slice(head * HSIZE, (head + 1) * HSIZE)
-        vcols = slice(width + head * HSIZE, width + (head + 1) * HSIZE)
-        q = q_ref[:, cols]
-        g = g_ref[:, cols]
-        k = kv_ref[:, cols]
-        v = kv_ref[:, vcols]
-        scores = dot(q, k, ((1,), (1,))) * scale
-        dprob = dot(g, v, ((1,), (1,)))
-        expo = jnp.exp(scores - jnp.max(scores, axis=-1, keepdims=True))
-        prob = expo * (1.0 / jnp.sum(expo, axis=-1, keepdims=True))
-        prob_b = prob.astype(jnp.bfloat16)
-        rowdot = jnp.sum(prob * dprob, axis=-1, keepdims=True)
-        dscore = (prob * (dprob - rowdot) * scale).astype(jnp.bfloat16)
-        out_ref[:, cols] = dot(prob_b, v, ((1,), (0,))).astype(jnp.bfloat16)
-        dq_ref[:, cols] = dot(dscore, k, ((1,), (0,))).astype(jnp.bfloat16)
-        both_ref[:, cols] = dot(dscore, q, ((0,), (0,))).astype(jnp.bfloat16)
-        both_ref[:, vcols] = dot(prob_b, g, ((0,), (0,))).astype(jnp.bfloat16)
-
-
-def attend(block_q, block_g, kv, stretches):
+    bf = jnp.bfloat16
+    states = jnp.concatenate([ref[0] for ref in state_refs], axis=0)
+    lt_ref[...] = dot(shuffle_ref[...], states, ((0,), (1,))).astype(bf)
+    for first in range(0, width // HSIZE, group):
+        many = slice(first * HSIZE, (first + group) * HSIZE)
+        vmany = slice(width + first * HSIZE, width + (first + group) * HSIZE)
+        keys = dot(states, w_ref[:, many], ((1,), (0,))).astype(bf)
+        values = dot(states, w_ref[:, vmany], ((1,), (0,))).astype(bf)
+        heads = range(group)
+        local = [slice(h * HSIZE, (h + 1) * HSIZE) for h in heads]
+        cols = [slice((first + h) * HSIZE, (first + h + 1) * HSIZE) for h in heads]
+        vcols = [slice(width + (first + h) * HSIZE, width + (first + h + 1) * HSIZE) for h in heads]
+        q = [q_ref[:, cols[h]] for h in heads]
+        g = [g_ref[:, cols[h]] for h in heads]
+        k = [keys[:, local[h]] for h in heads]
+        v = [values[:, local[h]] for h in heads]
+        scores = [dot(q[h], k[h], ((1,), (1,))) * scale for h in heads]
+        dprob = [dot(g[h], v[h], ((1,), (1,))) for h in heads]
+        expo = [jnp.exp(t - jnp.max(t, axis=-1, keepdims=True)) for t in scores]
+        prob = [t * (1.0 / jnp.sum(t, axis=-1, keepdims=True)) for t in expo]
+        rowdot = [jnp.sum(prob[h] * dprob[h], axis=-1, keepdims=True) for h in heads]
+        dscore = [(prob[h] * (dprob[h] - rowdot[h]) * scale).astype(bf) for h in heads]
+        prob_b = [t.astype(bf) for t in prob]
+        for h in heads:
+            out_ref[:, cols[h]] = dot(prob_b[h], v[h], ((1,), (0,))).astype(bf)
+            dq_ref[:, cols[h]] = dot(dscore[h], k[h], ((1,), (0,))).astype(bf)
+        for h in heads:
+            both_ref[:, cols[h]] = dot(dscore[h], q[h], ((0,), (0,))).astype(bf)
+            both_ref[:, vcols[h]] = dot(prob_b[h], g[h], ((0,), (0,))).astype(bf)
+
+
+def attend(block_q, block_g, returned, slot_pos, w_both, shuffle, stretches):
     rows, width = block_q.shape
     length = rows // stretches
-    span = kv.shape[0] // stretches
+    asks = slot_pos.shape[0]
+    neigh = asks // stretches
+    _, nb_len, enc = returned.shape
+    span = neigh * nb_len
     scale = 1.0 / math.sqrt(HSIZE)
-    small = pl.BlockSpec((length, width), lambda u: (u, 0))
-    large = pl.BlockSpec((span, 2 * width), lambda u: (u, 0))
+    small = pl.BlockSpec((length, width), lambda u, slots: (u, 0))
+    large = pl.BlockSpec((span, 2 * width), lambda u, slots: (u, 0))
+    whole = lambda a: pl.BlockSpec(a.shape, lambda u, slots: (0, 0))
+    fetched = [
+        pl.BlockSpec((1, nb_len, enc), lambda u, slots, n=n: (slots[u * neigh + n], 0, 0))
+        for n in range(neigh)
+    ]
     return pl.pallas_call(
-        functools.partial(attend_kernel, scale),
-        grid=(stretches,),
-        in_specs=[small, small, large],
-        out_specs=[small, small, large],
+        functools.partial(attend_kernel, scale, 4),
+        grid_spec=pltpu.PrefetchScalarGridSpec(
+            num_scalar_prefetch=1,
+            grid=(stretches,),
+            in_specs=[small, small] + fetched + [whole(w_both), whole(shuffle)],
+            out_specs=[small, small, large, pl.BlockSpec((enc, span), lambda u, slots: (0, u))],
+        ),
         out_shape=[
             jax.ShapeDtypeStruct((rows, width), jnp.bfloat16),
             jax.ShapeDtypeStruct((rows, width), jnp.bfloat16),
-            jax.ShapeDtypeStruct(kv.shape, jnp.bfloat16),
+            jax.ShapeDtypeStruct((asks * nb_len, 2 * width), jnp.bfloat16),
+            jax.ShapeDtypeStruct((enc, asks * nb_len), jnp.bfloat16),
         ],
-        compiler_params=pltpu.CompilerParams(vmem_limit_bytes=40 << 20),
+        compiler_params=pltpu.CompilerParams(vmem_limit_bytes=48 << 20),
         cost_estimate=pl.CostEstimate(
-            flops=12 * rows * span * width,
-            bytes_accessed=8 * rows * width + 8 * kv.shape[0] * width,
+            flops=12 * rows * span * width + 4 * asks * nb_len * enc * width,
+            bytes_accessed=8 * rows * width + 8 * asks * nb_len * width,
             transcendentals=rows * span * width // HSIZE,
         ),
-    )(block_q, block_g, kv)
+    )(slot_pos, block_q, block_g, *[returned] * neigh, w_both, shuffle)
 
 
 def halve(block, axis, bit):
@@ -97,11 +122,11 @@
 
 
 def finish_kernel(
-    piece, lt_any, both_any, w_any, member_any, spread_ref,
+    piece, lt_any, both_any, w_any, ids_ref, spread_ref,
     gk_ref, gv_ref, gd_ref,
-    lt, both, wts, member, grad, got1, got2, got3, zed, got4, got5,
+    lt, both, wts, idbox, member, grad, got1, got2, got3, zed, got4, got5,
     dsend, arrived, give, dgot1, mine, xgive, dgot2,
-    load_sem, send_sem, recv_sem, asend_sem, arecv_sem,
+    load_sem, send_sem, recv_sem, asend_sem, arecv_sem, isend_sem, irecv_sem,
 ):
     bf, f32 = jnp.bfloat16, jnp.float32
     mesh_ids = pl.DeviceIdType.MESH
@@ -116,10 +141,9 @@
     pz1 = (dp + 4 - 8 * z1, db)
     others = [(lax.rem(dp + d, seqs), db) for d in range(1, seqs)]
     loads = [
-        pltpu.make_async_copy(lt_any, lt, load_sem.at[0]),
         pltpu.make_async_copy(both_any, both, load_sem.at[1]),
         pltpu.make_async_copy(w_any, wts, load_sem.at[2]),
-        pltpu.make_async_copy(member_any, member, load_sem.at[3]),
+        pltpu.make_async_copy(lt_any, lt, load_sem.at[0]),
     ]
     for load in loads:
         load.start()
@@ -168,35 +192,64 @@
             for j in range(2):
                 grad[p, c, i, j] = add(grad[p, c, i, j], got1[p, i, j])
 
-    asked = dsend.shape[2] // piece
-    rows = both.shape[0] // 2
+    asked = dsend.shape[1] // piece
+    total = both.shape[0]
+    enc = dsend.shape[2]
+    cuts = [slice(0, 512), slice(512, enc)]
 
     def states_grad(h):
-        out = lax.dot_general(
-            both[h * rows : (h + 1) * rows], wts[...], (((1,), (1,)), ((), ())),
-            preferred_element_type=f32,
-        ).astype(bf)
-        for r in range(asked):
-            for j in range(seqs):
-                start = (r * seqs + j) * piece
-                dsend[h, j, r * piece : (r + 1) * piece] = out[start : start + piece]
-        arrived[dp, h] = dsend[h, dp]
+        cols = cuts[h]
+        for part in range(2):
+            rows = total // 2
+            out = dot(both[part * rows : (part + 1) * rows], wts[cols], ((1,), (1,))).astype(bf)
+            for r in range(asked // 2):
+                into = (part * asked // 2 + r) * piece
+                for j in range(seqs):
+                    start = (r * seqs + j) * piece
+                    dsend[j, into : into + piece, cols] = out[start : start + piece]
+        arrived[dp, :, cols] = dsend[dp, :, cols]
         return [
-            send(dsend.at[h, peer[0]], arrived.at[dp, h], peer, (h, d))
+            send(dsend.at[peer[0], :, cols], arrived.at[dp, :, cols], peer, (h, d))
             for d, peer in enumerate(others)
         ]
 
+    idbox[dp] = ids_ref[...]
+    named = []
+    for d, peer in enumerate(others):
+        copy = pltpu.make_async_remote_copy(
+            src_ref=ids_ref,
+            dst_ref=idbox.at[dp],
+            send_sem=isend_sem.at[d],
+            recv_sem=irecv_sem.at[d],
+            device_id=peer,
+            device_id_type=mesh_ids,
+        )
+        copy.start()
+        named.append(copy)
     loads[0].wait()
     loads[1].wait()
+    across = [states_grad(0), states_grad(1)]
+    loads[2].wait()
     key1 = weight_grad(0)
-    loads[2].wait()
-    across = states_grad(0)
+    value1 = weight_grad(1)
     after_core(0, key1)
     key2 = send(grad.at[0, c, 1 - x], got2.at[0], px)
-    across += states_grad(1)
-    value1 = weight_grad(1)
     after_core(1, value1)
     value2 = send(grad.at[1, c, :, 1 - y], got2.at[1], py)
+
+    block = gd_ref.shape[0]
+    lanes = member.shape[1] // seqs
+    for copy in named:
+        copy.wait_recv()
+    row = lax.broadcasted_iota(jnp.int32, (block, lanes), 0)
+    lane = lax.broadcasted_iota(jnp.int32, (block, lanes), 1)
+    place = jnp.where(row % piece == lane % piece, row // piece, -1)
+    for i in range(member.shape[0] // block):
+        for k in range(seqs):
+            hit = place == idbox[k][0:1] - i * (block // piece)
+            member[i * block : (i + 1) * block, k * lanes : (k + 1) * lanes] = jnp.where(
+                hit & (place >= 0), 1.0, 0.0
+            ).astype(bf)
 
     def expand(p, total):
         zed[p] = (
@@ -219,30 +272,37 @@
     value3.wait_recv()
     value4 = expand(1, add(grad[1, c, x, y], got3[1]))
 
-    for copy in across:
-        copy.wait_recv()
-    loads[3].wait()
-    block = gd_ref.shape[0]
-    every = arrived.shape[0] * arrived.shape[1] * arrived.shape[2]
-
-    def dense(shard):
+    every = arrived.shape[0] * arrived.shape[1]
+
+    def dense(shard, cols):
         return jnp.dot(
             member[pl.ds(pl.multiple_of(shard * block, block), block)],
-            arrived[...].reshape(every, arrived.shape[3]),
+            arrived[:, :, cols].reshape(every, cols.stop - cols.start),
             preferred_element_type=f32,
         )
 
-    core = []
-    for far in (1, 0):
-        side = x if far == 0 else 1 - x
-        give[far] = dense(2 * side + 1 - c).astype(bf)
-        core.append(send(give.at[far], dgot1.at[far], pc))
-    for far in (1, 0):
-        side = x if far == 0 else 1 - x
-        mine[far] = dense(2 * side + c)
-    core[0].wait_recv()
-    xgive[...] = (mine[1] + dgot1[1].astype(f32)).astype(bf)
-    xcopy = send(xgive, dgot2, px)
+    def core_start(h):
+        cols = cuts[h]
+        for copy in across[h]:
+            copy.wait_recv()
+        started = []
+        for far in (1, 0):
+            side = x if far == 0 else 1 - x
+            give[far, :, cols] = dense(2 * side + 1 - c, cols).astype(bf)
+            started.append(send(give.at[far, :, cols], dgot1.at[far, :, cols], pc))
+        for far in (1, 0):
+            side = x if far == 0 else 1 - x
+            mine[far, :, cols] = dense(2 * side + c, cols)
+        return started
+
+    def x_start(h, started):
+        cols = cuts[h]
+        started[0].wait_recv()
+        xgive[:, cols] = (mine[1, :, cols] + dgot1[1, :, cols].astype(f32)).astype(bf)
+        copy = send(xgive.at[:, cols], dgot2.at[:, cols], px)
+        started[1].wait_recv()
+        mine[0, :, cols] = mine[0, :, cols] + dgot1[0, :, cols].astype(f32)
+        return copy
 
     def last(p, copy):
         copy.wait_recv()
@@ -250,33 +310,35 @@
             zed[p, z0, j] = add(zed[p, z0, j], got4[p, j])
         return send(zed.at[p, z0, 1 - z1], got5.at[p], pz1)
 
+    xcopy = [x_start(0, core_start(0))]
     key5 = last(0, key4)
     value5 = last(1, value4)
-    core[1].wait_recv()
-    mine[0] = mine[0] + dgot1[0].astype(f32)
+    xcopy.append(x_start(1, core_start(1)))
     for p, copy, out_ref in ((0, key5, gk_ref), (1, value5, gv_ref)):
         copy.wait_recv()
-        total = zed[p, z0, z1].astype(f32) + got5[p].astype(f32)
-        out_ref[...] = total[: out_ref.shape[0]]
-    xcopy.wait_recv()
-    gd_ref[...] = (mine[0] + dgot2[...].astype(f32)).astype(bf)
-    for copy in copies + across:
+        summed = zed[p, z0, z1].astype(f32) + got5[p].astype(f32)
+        out_ref[...] = summed[: out_ref.shape[0]]
+    for h in range(2):
+        xcopy[h].wait_recv()
+        cols = cuts[h]
+        gd_ref[:, cols] = (mine[0, :, cols] + dgot2[:, cols].astype(f32)).astype(bf)
+    for copy in copies + across[0] + across[1] + named:
         copy.wait_send()
 
 
-def finish(lt, both, w_both, member, spread, share, seqs, block, piece):
+def finish(lt, both, w_both, ids, spread, share, shards, seqs, block, piece):
     enc, rows = lt.shape
     wide = both.shape[1]
     half = wide // 2
     quarter = enc // 8
     padded = spread.shape[0] // 4
     bf = jnp.bfloat16
-    own = member.shape[1] // seqs
+    own = ids.shape[1]
     anywhere = pl.BlockSpec(memory_space=pl.ANY)
     vmem = pl.BlockSpec(memory_space=pltpu.VMEM)
     return pl.pallas_call(
         functools.partial(finish_kernel, piece),
-        in_specs=[anywhere] * 4 + [vmem],
+        in_specs=[anywhere] * 3 + [vmem] * 2,
         out_specs=[vmem] * 3,
         out_shape=[
             jax.ShapeDtypeStruct((share, half), jnp.float32),
@@ -287,7 +349,8 @@
             pltpu.VMEM(lt.shape, bf),
             pltpu.VMEM(both.shape, bf),
             pltpu.VMEM(w_both.shape, bf),
-            pltpu.VMEM(member.shape, bf),
+            pltpu.VMEM((seqs,) + ids.shape, jnp.int32),
+            pltpu.VMEM((shards * block, seqs * own), bf),
             pltpu.VMEM((2, 2, 2, 2, quarter, half), bf),
             pltpu.VMEM((2, 2, 2, quarter, half), bf),
             pltpu.VMEM((2, 2, quarter, half), bf),
@@ -295,23 +358,25 @@
             pltpu.VMEM((2, 2, 2, padded, half), bf),
             pltpu.VMEM((2, 2, padded, half), bf),
             pltpu.VMEM((2, padded, half), bf),
-            pltpu.VMEM((2, seqs, own // 2, enc), bf),
-            pltpu.VMEM((seqs, 2, own // 2, enc), bf),
+            pltpu.VMEM((seqs, own, enc), bf),
+            pltpu.VMEM((seqs, own, enc), bf),
             pltpu.VMEM((2, block, enc), bf),
             pltpu.VMEM((2, block, enc), bf),
             pltpu.VMEM((2, block, enc), jnp.float32),
             pltpu.VMEM((block, enc), bf),
             pltpu.VMEM((block, enc), bf),
-            pltpu.SemaphoreType.DMA((4,)),
+            pltpu.SemaphoreType.DMA((3,)),
             pltpu.SemaphoreType.DMA((16,)),
             pltpu.SemaphoreType.DMA((16,)),
             pltpu.SemaphoreType.DMA((2, seqs - 1)),
             pltpu.SemaphoreType.DMA((2, seqs - 1)),
+            pltpu.SemaphoreType.DMA((seqs - 1,)),
+            pltpu.SemaphoreType.DMA((seqs - 1,)),
         ],
         compiler_params=pltpu.CompilerParams(
             vmem_limit_bytes=62 << 20, collective_id=0, has_side_effects=True
         ),
-    )(lt, both, w_both, member, spread)
+    )(lt, both, w_both, ids, spread)
 
 
 def body(queries, cotangent, w_key, w_value, database, nb_shard, nb_row):
@@ -341,8 +406,7 @@
     held, w_key, w_value, target, wanted = lax.optimization_barrier(
         (picked, w_key, w_value, target, wanted)
     )
-    ids = jnp.broadcast_to((target * db_count + wanted)[None], (seqs, asks))
-    ids = lax.all_to_all(ids, "dp", split_axis=0, concat_axis=0, tiled=True).reshape(seqs * asks)
+    own_ids = target * db_count + wanted
     w_both = jnp.concatenate([w_key, w_value], axis=1)
     returned = lax.all_to_all(held, "db", split_axis=0, concat_axis=0, tiled=True)
 
@@ -359,11 +423,8 @@
     piece = nb_len // seqs
     fused = shards == 4 and seqs == 8
     if fused:
-        row = jnp.arange(shards * db_count * piece, dtype=jnp.int32)[:, None]
-        col = jnp.arange(seqs * asks * piece, dtype=jnp.int32)[None, :]
-        member = (
-            (jnp.broadcast_to(ids[:, None], (seqs * asks, piece)).reshape(1, -1) == row // piece) & (row % piece == col % piece)
-        ).astype(jnp.bfloat16)
+        ids = jnp.broadcast_to(own_ids[:, None], (asks, piece)).reshape(1, asks * piece)
+        ids = jnp.broadcast_to(ids, (8, asks * piece))
         padded = -(-share // 16) * 16
         row = jnp.arange(4 * padded, dtype=jnp.int32)[:, None]
         col = jnp.arange(4 * share, dtype=jnp.int32)[None, :]
@@ -371,14 +432,17 @@
             jnp.bfloat16
         )
     else:
+        ids = jnp.broadcast_to(own_ids[None], (seqs, asks))
+        ids = lax.all_to_all(ids, "dp", split_axis=0, concat_axis=0, tiled=True)
+        ids = ids.reshape(seqs * asks)
         member = (
             ids[None, :] == jnp.arange(shards * db_count, dtype=jnp.int32)[:, None]
         ).astype(jnp.bfloat16)
 
-    states = jnp.take(returned.reshape(shards * slot_count, nb_len, enc_width), slot_pos, axis=0, mode="clip")
-    states = states.reshape(asks * nb_len, enc_width)
-    kv = dot(states, w_both, ((1,), (0,))).astype(jnp.bfloat16)
-    outputs, dquery, both = attend(block_q, block_g, kv, stretch_count)
+    returned = returned.reshape(shards * slot_count, nb_len, enc_width)
+    outputs, dquery, both, lt = attend(
+        block_q, block_g, returned, slot_pos, w_both, shuffle, stretch_count
+    )
 
     keep = rows_local - span + 1
     prev_out, prev_dq = from_behind((outputs[keep:], dquery[keep:]), "db", 1)
@@ -386,18 +450,16 @@
     grad_queries = jnp.concatenate([prev_dq, dquery[:keep]], axis=0)[None]
 
     if fused:
-        shuffled = dot(shuffle, states, ((0,), (1,))).astype(jnp.bfloat16)
         *grads, grad_database = finish(
-            shuffled, both, w_both, member, spread, share, seqs, db_count * piece, piece
+            lt, both, w_both, ids, spread, share, shards, seqs, db_count * piece, piece
         )
         grad_database = grad_database.reshape(db_count, piece, enc_width)
         return (attn_out, grad_queries, grads[0], grads[1], grad_database)
 
-    shuffled = dot(states, shuffle, ((1,), (0,))).astype(jnp.bfloat16)
     steps = [("db", b) for b in bits_of("db")] + [("dp", b) for b in bits_of("dp")]
     grads = []
     for part in range(2):
-        grad = dot(shuffled, both[:, part * width : (part + 1) * width], ((0,), (0,)))
+        grad = dot(lt, both[:, part * width : (part + 1) * width], ((1,), (0,)))
         grads.append(halve_all(grad.astype(jnp.bfloat16), steps))
     dstates = dot(both, w_both, ((1,), (1,))).astype(jnp.bfloat16)
     dstates = dstates.reshape(asks, seqs, piece, enc_width).transpose(1, 0, 2, 3)

time: 237 us -> 208 us (0.88)
  matrix products: 17.1 us -> 0 us
  starting transfers between devices: 22.3 us -> 16.2 us
  waiting for transfers between devices: 27 us -> 22.9 us
    dot_general x2 -> x0, matrix products: 17.1 us -> none  [dot(): lax.dot_general(a, b, (dims, ((), ())), preferred_element_type=jnp.float32)]
    all_to_all x1 -> x0, waiting for transfers between devices: 6.37 us -> none  [body(): lax.all_to_all(ids, 'dp', split_axis=0, concat_axis=0, tiled=True)]
    all_to_all x1 -> x0, starting transfers between devices: 6.31 us -> none  [body(): lax.all_to_all(ids, 'dp', split_axis=0, concat_axis=0, tiled=True)]
    pallas_call x1, Pallas kernels: 96.1 us -> 101 us  [finish(): pl.pallas_call(functools.partial(finish_kernel, piece), in_specs=[anywher...]
    pallas_call x1, Pallas kernels: 32 us -> 27.2 us  [attend(): pl.pallas_call(functools.partial(attend_kernel, scale, 4), grid_spec=pltp...]
    gather x1 -> x0, local copies, waits for them, and re-layouts: 3.79 us -> none  [body(): jnp.take(returned.reshape(shards * slot_count, nb_len, enc_width), slot_p...]
    unnamed x22 -> x24, local copies, waits for them, and re-layouts: 8.5 us -> 11.8 us
  transfers between devices with their start and end apart: 7 -> 6, of which waited for: 2 -> 1; matrix products, arithmetic and copies ran while one was open for 13% -> 14% of each run, Pallas kernels for 41% -> 49%
where the time goes in v2:
time: 208 us
  Pallas kernels  128 us (62%)
  local copies, waits for them, and re-layouts  29.1 us (14%)
  waiting for transfers between devices  22.9 us (11%)
  starting transfers between devices  16.2 us (8%)
  other arithmetic  10.5 us (5%)
    pallas_call x1, Pallas kernels, finish(): pl.pallas_call(functools.partial(finish_kernel, piece), in_specs=[anywher...  101 us
    pallas_call x1, Pallas kernels, attend(): pl.pallas_call(functools.partial(attend_kernel, scale, 4), grid_spec=pltp...  27.2 us
    all_to_all x1, waiting for transfers between devices, body(): lax.all_to_all(held, 'db', split_axis=0, concat_axis=0, tiled=True)  22.9 us
    unnamed x24, local copies, waits for them, and re-layouts  11.8 us
    ppermute x4, starting transfers between devices, from_behind(): return lax.ppermute(block, axis, route)  7.12 us
    gather x1, local copies, waits for them, and re-layouts, body(): picked = jnp.take(database, asked, axis=0, mode='clip')  5.65 us
    all_to_all x1, starting transfers between devices, body(): lax.all_to_all(held, 'db', split_axis=0, concat_axis=0, tiled=True)  4.9 us
    all_to_all x1, starting transfers between devices, body(): lax.all_to_all(send_ids, 'db', split_axis=0, concat_axis=0, tiled=True)  4.21 us
  transfers between devices with their start and end apart: 6, of which 1 were waited for; matrix products, arithmetic and copies ran while one was open for 14% of the time, Pallas kernels for 49%

profile of v2, /device:TPU:0, one launch (start us, length us, event | category | flops | bytes accessed | tf_op | source)
XLA Modules:
  0.0 207.7 jit_solution(9776358914588213768)
XLA Ops:
  0.6 0.8 copy.20
  1.4 0.1 reshape_squeeze.4
  1.5 0.2 reduce_window_sum.11
  1.7 0.8 copy.21
  2.5 0.1 mul.25
  2.6 0.1 select_reduce_fusion
  2.6 0.7 all_to_all.9
  3.3 4.2 %all-to-all-start = ((s32[4,1,3]{2,1,0:T(1,128)}), s32[4,1,3]{2,1,0:T(1,128)S(1)}, u32[]{:S(2)}, u32[]{:S(2)}) async-start(s32[4,1,3]{2,1,0:T(1,128)} %bitcast.4), calls=%async_computation | async-start | bytes 4096 | tf_op jit(solution)/shard_map/all_to_all | solution.py:404
  7.5 1.0 slice_bitcast_fusion.3
  8.5 1.3 collective-permute-start
  9.8 1.0 slice_bitcast_fusion.2
  10.8 1.3 collective-permute-start.1
  12.1 1.3 fusion.refs_3_
  13.4 0.0 all-to-all-done
  13.4 0.5 broadcast.140
  13.9 0.7 reduce.3
  14.6 0.1 reshape.130
  14.6 5.6 %gather_fusion = bf16[12,128,896]{2,1,0:T(8,128)(2,1)} fusion(bf16[32,128,896]{2,1,0:T(8,128)(2,1)} %param.12, s32[1024]{0:T(1024)S(1)} %pad_clamp_fusion), kind=kCustom, calls=%fused_computation | custom fusion | bytes 5505072 | tf_op jit(solution)/shard_map/jit(_take)/gather | solution.py:405
  20.3 0.0 copy-start.5
  20.3 4.9 %all-to-all-start.1 = ((bf16[4,3,128,896]{3,2,1,0:T(8,128)(2,1)}), bf16[4,3,128,896]{3,2,1,0:T(8,128)(2,1)}, u32[]{:S(2)}, u32[]{:S(2)}) async-start(bf16[4,3,128,896]{3,2,1,0:T(8,128)(2,1)} %bitcast.18), calls=%async_computation.1 | async-start | bytes 5505024 | tf_op jit(solution)/shard_map/all_to_all | solution.py:411
  25.2 0.0 copy-done.5
  25.2 0.2 slice_bitcast_fusion.1
  25.4 1.3 slice_bitcast_fusion
  26.8 0.0 copy-start.3
  26.8 4.5 %constant_dynamic-update-slice_fusion.1 = bf16[896,4096]{1,0:T(8,128)(2,1)} fusion(bf16[896,2048]{1,0:T(8,128)(2,1)} %param.10), kind=kLoop, calls=%fused_computation.14 | loop fusion | bytes 7340032
  31.2 0.0 copy-done.3
  31.2 2.3 %constant_dynamic-update-slice_fusion.refs_2_.w_any = bf16[896,4096]{1,0:T(8,128)(2,1)} fusion(bf16[896,4096]{1,0:T(8,128)(2,1)} %constant_dynamic-update-slice_fusion.1, bf16[896,2048]{1,0:T(8,128)(2,1)S(1)} %copy-done.3), kind=kLoop, calls=%fused_computation.13 | loop fusion | bytes 7340032 | tf_op jit(solution)/shard_map/concatenate | solution.py:410
  33.5 0.0 collective-permute-done
  33.5 2.1 pad_maximum_fusion.q_ref
  35.6 0.0 collective-permute-done.1
  35.6 1.1 pad_maximum_fusion.1.g_ref
  36.7 22.9 %all-to-all-done.1 = bf16[4,3,128,896]{3,2,1,0:T(8,128)(2,1)} async-done(((bf16[4,3,128,896]{3,2,1,0:T(8,128)(2,1)}), bf16[4,3,128,896]{3,2,1,0:T(8,128)(2,1)}, u32[]{:S(2)}, u32[]{:S(2)}) %all-to-all-start.1) | async-done | bytes 2752544 | tf_op jit(solution)/shard_map/all_to_all | solution.py:411
  59.5 0.0 copy-start.1
  59.6 1.2 copy-done.1
  60.8 0.0 copy-start.2
  60.8 1.2 copy-done.2
  62.0 27.2 %shard_map.119 = (bf16[256,2048]{1,0:T(8,128)(2,1)S(1)}, bf16[256,2048]{1,0:T(8,128)(2,1)S(1)}, bf16[1024,4096]{1,0:T(8,128)(2,1)}, bf16[896,1024]{1,0:T(8,128)(2,1)}) custom-call(s32[8]{0:T(128)S(1)} %multiply_add_fusion.1.slot_ref, bf16[256,2048]{1,0:T(8,128)(2,1)S(1)} %copy-done.1, bf16[256,2048]{1,0:T(8,128)(2,1)S(1)} %copy-done.2, ...), custom_call_target="tpu_custom_call" | custom-call | flops 9126805504 | bytes 20971520 | tf_op jit(solution)/shard_map/pallas_call | solution.py:75
  89.2 0.0 copy-start
  89.2 1.0 copy-done
  90.1 0.8 slice.54
  90.9 2.5 %collective-permute-start.3 = (bf16[63,2048]{1,0:T(8,128)(2,1)}, bf16[63,2048]{1,0:T(8,128)(2,1)}, u32[]{:S(2)}, u32[]{:S(2)}) collective-permute-start(bf16[63,2048]{1,0:T(8,128)(2,1)} %slice.54), channel_id=1, source_target_pairs={{0,1},{1,2},{2,3},{4,5},{5,6},{6,7},{8,9},{9,10},{10,11},{12,13},{... | collective-permute-start | bytes 774152 | tf_op jit(solution)/shard_map/ppermute | solution.py:18
  93.4 0.7 and_convert_fusion.spread_ref
  94.2 0.8 slice.52
  94.9 2.0 collective-permute-start.2
  96.9 0.1 broadcast_in_dim.17
  97.0 0.1 broadcast_in_dim.34
  97.1 2.1 %slice.55 = bf16[193,2048]{1,0:T(8,128)(2,1)} slice(bf16[256,2048]{1,0:T(8,128)(2,1)} %copy-done), slice={[0:193], [0:2048]} | slice | bytes 1581056 | tf_op jit(solution)/shard_map/slice | solution.py:450
  99.2 0.1 slice.53
  99.3 0.6 broadcast_in_dim.35.ids_ref
  99.9 101.1 %shard_map.120 = (f32[28,2048]{1,0:T(8,128)}, f32[28,2048]{1,0:T(8,128)}, bf16[512,896]{1,0:T(8,128)(2,1)}) custom-call(bf16[896,1024]{1,0:T(8,128)(2,1)} %get-tuple-element.22.lt_any, bf16[1024,4096]{1,0:T(8,128)(2,1)} %get-tuple-element.23.both_any, bf16[896,4096]{1,0:T(8,128)(2,1)} %constant_dynamic-update-slice_fusion.refs_2_.w_any, ...), custom_call_target="tpu_custom_call" | custom-call | tf_op jit(solution)/shard_map/pallas_call | solution.py:339
  201.0 0.0 copy-start.8
  201.0 0.0 copy-start.7
  201.0 0.0 copy-start.6
  201.0 0.0 collective-permute-done.3
  201.0 0.0 copy-done.4
  201.0 2.2 %maximum_bitcast_fusion.1 = bf16[1,256,2048]{2,1,0:T(8,128)(2,1)} fusion(bf16[193,2048]{1,0:T(8,128)(2,1)S(1)} %copy-done.4, bf16[63,2048]{1,0:T(8,128)(2,1)} %collective-permute-done.3), kind=kLoop, calls=%fused_computation.6 | loop fusion | flops 2097152 | bytes 2097152 | tf_op jit(solution)/shard_map/broadcast_in_dim | solution.py:450
  203.2 0.0 collective-permute-done.2
  203.2 2.1 %maximum_bitcast_fusion = bf16[1,256,2048]{2,1,0:T(8,128)(2,1)} fusion(bf16[193,2048]{1,0:T(8,128)(2,1)S(1)} %slice.53, bf16[63,2048]{1,0:T(8,128)(2,1)} %collective-permute-done.2), kind=kLoop, calls=%fused_computation.5 | loop fusion | flops 2097152 | bytes 2097152 | tf_op jit(solution)/shard_map/broadcast_in_dim | solution.py:449
  205.4 0.0 copy-done.8
  205.4 0.7 copy.27
  206.1 0.0 copy-done.7
  206.1 0.7 copy.28
  206.8 0.0 copy-done.6
  206.8 0.9 copy.29
  (8 shorter events, 0.1 us)
Async XLA Ops:
  3.3 10.1 %all-to-all-start = ((s32[4,1,3]{2,1,0:T(1,128)}), s32[4,1,3]{2,1,0:T(1,128)S(1)}, u32[]{:S(2)}, u32[]{:S(2)}) async-start(s32[4,1,3]{2,1,0:T(1,128)} %bitcast.4), calls=%async_computation | async-start | bytes 4096 | tf_op jit(solution)/shard_map/all_to_all | solution.py:404
  8.5 25.0 %collective-permute-start = (bf16[64,2048]{1,0:T(8,128)(2,1)S(1)}, bf16[64,2048]{1,0:T(8,128)(2,1)}, u32[]{:S(2)}, u32[]{:S(2)}) collective-permute-start(bf16[64,2048]{1,0:T(8,128)(2,1)S(1)} %slice_bitcast_fusion.3), channel_id=1, source_target_pairs={{1,0},{2,1},{3,2},{5,4},{6,5},{7,6},{9,8},{10,9},{11,10},{13,12},{... | collective-permute-start | bytes 786440 | tf_op jit(solution)/shard_map/ppermute | solution.py:18
  10.8 24.8 %collective-permute-start.1 = (bf16[64,2048]{1,0:T(8,128)(2,1)S(1)}, bf16[64,2048]{1,0:T(8,128)(2,1)S(1)}, u32[]{:S(2)}, u32[]{:S(2)}) collective-permute-start(bf16[64,2048]{1,0:T(8,128)(2,1)S(1)} %slice_bitcast_fusion.2), channel_id=1, source_target_pairs={{1,0},{2,1},{3,2},{5,4},{6,5},{7,6},{9,8},{10,9},{11,10},{13,12},{... | collective-permute-start | bytes 786440 | tf_op jit(solution)/shard_map/ppermute | solution.py:18
  20.3 4.9 %copy-start.5 = (bf16[1,256,2048]{2,1,0:T(8,128)(2,1)S(1)}, bf16[1,256,2048]{2,1,0:T(8,128)(2,1)}, u32[]{:S(2)}) copy-start(bf16[1,256,2048]{2,1,0:T(8,128)(2,1)} %param.8) | copy-start | bytes 3145732
  20.3 39.2 %all-to-all-start.1 = ((bf16[4,3,128,896]{3,2,1,0:T(8,128)(2,1)}), bf16[4,3,128,896]{3,2,1,0:T(8,128)(2,1)}, u32[]{:S(2)}, u32[]{:S(2)}) async-start(bf16[4,3,128,896]{3,2,1,0:T(8,128)(2,1)} %bitcast.18), calls=%async_computation.1 | async-start | bytes 5505024 | tf_op jit(solution)/shard_map/all_to_all | solution.py:411
  26.8 4.5 %copy-start.3 = (bf16[896,2048]{1,0:T(8,128)(2,1)S(1)}, bf16[896,2048]{1,0:T(8,128)(2,1)}, u32[]{:S(2)}) copy-start(bf16[896,2048]{1,0:T(8,128)(2,1)} %param.11) | copy-start | bytes 11010052
  59.5 1.2 copy-start.1
  60.8 1.2 copy-start.2
  89.2 1.0 copy-start
  90.9 110.1 %collective-permute-start.3 = (bf16[63,2048]{1,0:T(8,128)(2,1)}, bf16[63,2048]{1,0:T(8,128)(2,1)}, u32[]{:S(2)}, u32[]{:S(2)}) collective-permute-start(bf16[63,2048]{1,0:T(8,128)(2,1)} %slice.54), channel_id=1, source_target_pairs={{0,1},{1,2},{2,3},{4,5},{5,6},{6,7},{8,9},{9,10},{10,11},{12,13},{... | collective-permute-start | bytes 774152 | tf_op jit(solution)/shard_map/ppermute | solution.py:18
  94.9 108.3 %collective-permute-start.2 = (bf16[63,2048]{1,0:T(8,128)(2,1)}, bf16[63,2048]{1,0:T(8,128)(2,1)}, u32[]{:S(2)}, u32[]{:S(2)}) collective-permute-start(bf16[63,2048]{1,0:T(8,128)(2,1)} %slice.52), channel_id=1, source_target_pairs={{0,1},{1,2},{2,3},{4,5},{5,6},{6,7},{8,9},{9,10},{10,11},{12,13},{... | collective-permute-start | bytes 774152 | tf_op jit(solution)/shard_map/ppermute | solution.py:18
  99.9 101.1 %copy-start.4 = (bf16[193,2048]{1,0:T(8,128)(2,1)S(1)}, bf16[193,2048]{1,0:T(8,128)(2,1)}, u32[]{:S(2)}) copy-start(bf16[193,2048]{1,0:T(8,128)(2,1)} %slice.55) | copy-start | bytes 2371588
  201.0 4.4 %copy-start.8 = (f32[28,2048]{1,0:T(8,128)S(1)}, f32[28,2048]{1,0:T(8,128)}, u32[]{:S(2)}) copy-start(f32[28,2048]{1,0:T(8,128)} %get-tuple-element.40) | copy-start | bytes 688132
  201.0 5.1 %copy-start.7 = (f32[28,2048]{1,0:T(8,128)S(1)}, f32[28,2048]{1,0:T(8,128)}, u32[]{:S(2)}) copy-start(f32[28,2048]{1,0:T(8,128)} %get-tuple-element.41) | copy-start | bytes 688132
  201.0 5.8 %copy-start.6 = (bf16[512,896]{1,0:T(8,128)(2,1)S(1)}, bf16[512,896]{1,0:T(8,128)(2,1)}, u32[]{:S(2)}) copy-start(bf16[512,896]{1,0:T(8,128)(2,1)} %get-tuple-element.28) | copy-start | bytes 2752516
